TPU v7x, 32 devices: a whole 2x2x4 slice. The times are simulated.
32 devices in a mesh: row: 8 (over z, core), col: 4 (over y, x).
Axes of the slice: x: 2, y: 2, z: 4, core: 2. Of those that a mesh axis runs over, the one named last changes fastest.
Arguments:
- inverse_factor: float32 [32, 1024, 1024], P(('row', 'col')), as said below
- coupling: float32 [32, 1024, 768], P(('row', 'col'))
- boundary_stiffness: float32 [32, 768, 768], P(('row', 'col')), as said below
- interior_mass: float32 [32, 1024], P(('row', 'col')), may hold values from 0.5 to 2
- boundary_mass: float32 [32, 768], P(('row', 'col')), may hold values from 0.5 to 1
- interface_ids: int32 [32, 768], replicated, may hold values from 0 to 8191, as said below
- trial_modes: float32 [8192, 512], P('col'), may hold values from -4 to 4
Outputs:
- reduced_matrix: float32 [8192, 8192], P('row', 'col')
- reduced_columns: float32 [512, 8192], P('col', 'row')
Inputs may be any that keep to these rules, and one draw needn't show every extreme that they name: `interface_ids`: row s lists the 768 interface unknowns of substructure s as six distinct runs of 128 consecutive ids, each starting at a multiple of 128, runs in any order. With g = id // 128 the run's number, three runs of every list have g in one residue class modulo 2, the same class for all lists, and the other three are spread evenly over the other classes; every run number is listed by some substructure. `inverse_factor`: lower triangular with a positive diagonal. Symmetric, and boundary_stiffness[s] - W_s^T W_s is positive definite.
All inputs are finite; a program needn't handle non-finite values.
Results may differ from a plain program's by a relative error of at most 0.0001.
Values sent between devices are 32-bit elements; how exact they have to be, the bound alone decides.
No kernel may reach another device: no remote copies, remote signals or barrier semaphores. Data moves between devices by JAX's collectives and lax.ppermute only.
A program may use at most 192 MiB of HBM per device.

v0:
```python
import jax
import jax.numpy as jnp
from jax import lax
from jax.sharding import PartitionSpec as P

SUB = 32
NG = 8192
PANEL = 512


highest = lax.Precision.HIGHEST
shift_value = 0.05


def lower_solve(lower, rhs):
    return lax.linalg.triangular_solve(lower, rhs, left_side=True, lower=True)


def matmul(left, right):
    return jnp.dot(left, right, precision=highest)


def tmatmul(left, right):
    return lax.dot_general(left, right, (((0,), (0,)), ((), ())), precision=highest)


def tile_layout(blocks, row_count, col_count):
    row_residue = blocks % row_count
    col_residue = blocks % col_count
    number = blocks.shape[-1]
    earlier = jnp.arange(number)[None, :] < jnp.arange(number)[:, None]
    same_row = row_residue[..., :, None] == row_residue[..., None, :]
    same_col = col_residue[..., :, None] == col_residue[..., None, :]
    row_rank = jnp.sum(same_row & earlier, axis=-1)
    col_rank = jnp.sum(same_col & earlier, axis=-1)
    col_total = jnp.sum(same_col, axis=-1)
    target = row_residue[..., :, None] * col_count + col_residue[..., None, :]
    position = row_rank[..., :, None] * col_total[..., None, :] + col_rank[..., None, :]
    return (target, position)


def to_tiles(matrix, blocks_per_side):
    shaped = matrix.reshape(blocks_per_side, SUB, blocks_per_side, SUB).transpose(0, 2, 1, 3)
    return shaped.reshape(blocks_per_side * blocks_per_side, SUB * SUB)


def body(
    inverse_factor,
    coupling,
    boundary_stiffness,
    interior_mass,
    boundary_mass,
    interface_ids,
    trial_modes,
):
    row_count = lax.axis_size("row")
    col_count = lax.axis_size("col")
    classes = row_count // 4
    capacity = 3 * (3 + (row_count // col_count - 1) * (3 // (classes - 1)))
    sources = row_count * col_count
    row_blocks = NG // (SUB * row_count)
    col_blocks = NG // (SUB * col_count)
    factor = inverse_factor[0]
    link = coupling[0]
    weighted = matmul(factor, link)
    condensed_k = boundary_stiffness[0] - tmatmul(weighted, weighted)
    static = tmatmul(factor, weighted)
    condensed_m = jnp.diag(boundary_mass[0]) + tmatmul(static, interior_mass[0][:, None] * static)
    blocks_per_side = link.shape[1] // SUB
    payload = jnp.stack(
        [to_tiles(condensed_k, blocks_per_side), to_tiles(condensed_m, blocks_per_side)], axis=1
    )
    payload = payload.reshape(blocks_per_side * blocks_per_side, 2 * SUB * SUB)
    all_blocks = interface_ids[:, ::SUB] // SUB
    own_index = lax.axis_index("row") * col_count + lax.axis_index("col")
    own_blocks = lax.dynamic_index_in_dim(all_blocks, own_index, 0, keepdims=False)
    target, position = tile_layout(own_blocks, row_count, col_count)
    slot_of = (target * capacity + position).reshape(-1)
    send_pick = (
        jnp.arange(sources * capacity, dtype=jnp.int32)[:, None] == slot_of[None, :]
    ).astype(jnp.float32)
    outbox = matmul(send_pick, payload).reshape(sources, capacity, 2, SUB * SUB)
    inbox = lax.all_to_all(outbox, ("row", "col"), split_axis=0, concat_axis=0, tiled=True)
    inbox = inbox.reshape(sources * capacity, 2 * SUB * SUB)
    every_target, every_position = tile_layout(all_blocks, row_count, col_count)
    code = all_blocks[:, :, None] // row_count * col_blocks + all_blocks[:, None, :] // col_count
    slot_index = jnp.where(every_target == own_index, every_position, capacity)
    slot_hits = slot_index[..., None] == jnp.arange(capacity, dtype=jnp.int32)
    table = jnp.sum(jnp.where(slot_hits, code[..., None] + 1, 0), axis=(1, 2)) - 1
    recv_pick = (
        jnp.arange(row_blocks * col_blocks, dtype=jnp.int32)[:, None] == table.reshape(-1)[None, :]
    ).astype(jnp.float32)
    placed = matmul(recv_pick, inbox)
    local = (
        placed.reshape(row_blocks, col_blocks, 2, SUB, SUB)
        .transpose(2, 0, 3, 1, 4)
        .reshape(2, row_blocks * SUB, col_blocks * SUB)
    )
    mass_local = local[1]
    shifted = local[0] - shift_value * mass_local
    panel_row_count = PANEL // row_count
    panel_col_count = PANEL // col_count
    cols_gathered = lax.all_gather(shifted[:, :panel_col_count], "col", axis=1, tiled=True)
    panel_cols = (
        cols_gathered.reshape(-1, col_count, panel_col_count // SUB, SUB)
        .transpose(0, 2, 1, 3)
        .reshape(-1, PANEL)
    )
    rows_gathered = lax.all_gather(shifted[:panel_row_count, :], "row", axis=0, tiled=True)
    panel_rows = (
        rows_gathered.reshape(row_count, panel_row_count // SUB, SUB, -1)
        .transpose(1, 0, 2, 3)
        .reshape(PANEL, -1)
    )
    pieces = lax.all_gather(
        shifted[:panel_row_count, :panel_col_count].reshape(1, panel_row_count * panel_col_count),
        ("row", "col"),
        axis=0,
        tiled=True,
    )
    corner = pieces.reshape(
        row_count, col_count, panel_row_count // SUB, SUB, panel_col_count // SUB, SUB
    )
    corner = corner.transpose(2, 0, 3, 4, 1, 5).reshape(PANEL, PANEL)
    lower = jnp.linalg.cholesky(corner)
    left_solved = lower_solve(lower, panel_cols.T)
    right_solved = lower_solve(lower, panel_rows)
    reduced_matrix = shifted - tmatmul(left_solved, right_solved)
    modes_local = lax.psum_scatter(
        lax.dot_general(trial_modes, mass_local, (((0,), (1,)), ((), ())), precision=highest),
        "col",
        scatter_dimension=0,
        tiled=True,
    )
    panel_modes = lax.all_gather(modes_local[:, :panel_row_count], "row", axis=1, tiled=True)
    panel_modes = (
        panel_modes.reshape(-1, row_count, panel_row_count // SUB, SUB)
        .transpose(0, 2, 1, 3)
        .reshape(-1, PANEL)
    )
    modes_solved = lower_solve(lower, panel_modes.T)
    reduced_columns = modes_local - tmatmul(modes_solved, left_solved)
    return (reduced_matrix, reduced_columns)


def solution(mesh):
    return jax.shard_map(
        body,
        mesh=mesh,
        in_specs=(
            P(("row", "col"), None, None),
            P(("row", "col"), None, None),
            P(("row", "col"), None, None),
            P(("row", "col"), None),
            P(("row", "col"), None),
            P(),
            P("col", None),
        ),
        out_specs=(P("row", "col"), P("col", "row")),
        check_vma=False,
    )
```

profile of v0, /device:TPU:0, one launch (start us, length us, event | category | flops | bytes accessed | tf_op | source)
XLA Modules:
  0.0 701.2 jit_solution(10510201133354503019)
XLA Ops:
  9.2 12.6 %fusion.16 = f32[1024,768]{1,0:T(8,128)S(1)} fusion(f32[1,1024,1024]{2,1,0:T(8,128)} %param.7, f32[1,1024,768]{2,1,0:T(8,128)S(1)} %copy-done), kind=kOutput, calls=%fused_computation.26 | convolution fusion | flops 9663676416 | bytes 10485760 | tf_op jit(solution)/shard_map/dot_general | solution.py:20
  23.4 12.1 %fusion.14 = f32[768,1024]{1,0:T(8,128)} fusion(f32[1024,768]{1,0:T(8,128)S(1)} %fusion.16, f32[1,1024,1024]{2,1,0:T(8,128)S(1)} %copy-done.16), kind=kOutput, calls=%fused_computation.24 | convolution fusion | flops 9663676416 | bytes 10485760 | tf_op jit(solution)/shard_map/dot_general | solution.py:24
  35.6 10.8 %select_add_fusion = f32[768,768]{1,0:T(8,128)S(1)} fusion(f32[768,1024]{1,0:T(8,128)} %fusion.14, f32[1024]{0:T(1024)S(1)} %bitcast.185, f32[768]{0:T(1024)S(1)} %reduce.27), kind=kOutput, calls=%fused_computation.42 | convolution fusion | flops 7250313216 | bytes 5512192 | tf_op jit(solution)/shard_map/dot_general | solution.py:24
  51.4 9.0 %copy.137 = f32[24,32,24,32]{3,1,2,0:T(8,128)} copy(f32[24,32,24,32]{3,2,1,0:T(8,128)} %reshape.313) | data formatting | bytes 4718592 | tf_op jit(solution)/shard_map/reshape | solution.py:43
  60.4 8.4 %stack_reshape.7 = f32[576,1,1024]{2,0,1:T(8,128)} reshape(f32[24,24,32,32]{3,2,1,0:T(8,128)} %bitcast.164) | data formatting | bytes 4718592 | tf_op jit(solution)/shard_map/stack;reshape | solution.py:70
  68.7 11.1 %bitcast_subtract_fusion = f32[768,768]{1,0:T(8,128)} fusion(f32[1,768,768]{2,1,0:T(8,128)} %param.9, f32[1024,768]{1,0:T(8,128)S(1)} %copy-done.5), kind=kOutput, calls=%fused_computation.41 | convolution fusion | flops 7248347136 | bytes 7864320 | tf_op jit(solution)/shard_map/dot_general | solution.py:24
  79.8 6.9 reshape.312
  86.7 9.0 %copy.138 = f32[24,32,24,32]{3,1,2,0:T(8,128)} copy(f32[24,32,24,32]{3,2,1,0:T(8,128)} %reshape.312) | data formatting | bytes 4718592 | tf_op jit(solution)/shard_map/reshape | solution.py:43
  95.7 8.5 %stack_reshape.6 = f32[576,1,1024]{2,0,1:T(8,128)} reshape(f32[24,24,32,32]{3,2,1,0:T(8,128)} %bitcast.165) | data formatting | bytes 4718592 | tf_op jit(solution)/shard_map/stack;reshape | solution.py:70
  104.2 7.6 %fusion.4 = f32[32,18,2,1024]{3,0,2,1:T(8,128)S(1)} fusion(s32[576]{0:T(1024)S(1)} %add.237, s32[32,18]{0,1:T(8,128)S(1)} %multiply_add_fusion.1, f32[576,1,1024]{2,0,1:T(8,128)S(1)} %copy-done.12, f32[576,1,1024]{2,0,1:T(8,128)} %stack_reshape.6), kind=kOutput, calls=%fused_computation.13 | convolution fusion | flops 8155238400 | bytes 9441792 | tf_op jit(solution)/shard_map/dot_general | solution.py:20
  117.7 7.4 %all-to-all-start = ((f32[32,18,2,1024]{3,2,1,0:T(2,128)}), f32[32,18,2,1024]{3,2,1,0:T(2,128)}, u32[]{:S(2)}, u32[]{:S(2)}) async-start(f32[32,18,2,1024]{3,2,1,0:T(2,128)} %copy.109), calls=%async_computation | async-start | bytes 9437184 | tf_op jit(solution)/shard_map/all_to_all | solution.py:83
  126.5 104.6 %all-to-all-done = f32[32,18,2,1024]{3,2,1,0:T(2,128)} async-done(((f32[32,18,2,1024]{3,2,1,0:T(2,128)}), f32[32,18,2,1024]{3,2,1,0:T(2,128)}, u32[]{:S(2)}, u32[]{:S(2)}) %all-to-all-start) | async-done | bytes 4718624 | tf_op jit(solution)/shard_map/all_to_all | solution.py:83
  243.7 44.7 %convolution_bitcast_fusion = f32[2,32,32,64,32]{3,4,2,0,1:T(8,128)} fusion(f32[2,32,32,576,1]{3,2,1,0,4:T(8,128)} %bitcast.177, s32[576]{0:T(1024)S(1)} %sub.40, s32[32,64]{1,0:T(8,128)S(1)} %multiply_add_fusion), kind=kOutput, calls=%fused_computation.2 | convolution fusion | flops 28992208896 | bytes 21506304 | tf_op jit(solution)/shard_map/dot_general | solution.py:20
  288.5 21.3 %fusion.124 = (f32[1,32,32,64,32]{3,4,2,0,1:T(8,128)}, f32[1,32,32,64,32]{3,4,2,0,1:T(8,128)}) fusion(f32[2,32,32,64,32]{3,4,2,0,1:T(8,128)} %convolution_bitcast_fusion), kind=kLoop, calls=%fused_computation.214 | loop fusion | bytes 33554432 | tf_op jit(solution)/shard_map/slice | solution.py:99
  309.7 23.0 %copy.111 = f32[1,32,32,64,32]{4,3,2,1,0:T(8,128)} copy(f32[1,32,32,64,32]{3,4,2,0,1:T(8,128)} %get-tuple-element.45) | data formatting | bytes 16777216 | tf_op jit(solution)/shard_map/slice | solution.py:100
  332.8 25.3 %squeeze.24 = f32[1024,2048]{1,0:T(8,128)} reshape(f32[1,32,32,64,32]{4,3,2,1,0:T(8,128)} %copy.111) | data formatting | bytes 16777216 | tf_op jit(solution)/shard_map/squeeze | solution.py:100
  358.1 23.0 %copy.112 = f32[1,32,32,64,32]{4,3,2,1,0:T(8,128)} copy(f32[1,32,32,64,32]{3,4,2,0,1:T(8,128)} %get-tuple-element.44) | data formatting | bytes 16777216 | tf_op jit(solution)/shard_map/slice | solution.py:99
  381.1 25.7 %squeeze.25 = f32[1024,2048]{1,0:T(8,128)} reshape(f32[1,32,32,64,32]{4,3,2,1,0:T(8,128)} %copy.112) | data formatting | bytes 16777216 | tf_op jit(solution)/shard_map/squeeze | solution.py:99
  406.8 12.0 %multiply_subtract_fusion = f32[1024,2048]{1,0:T(8,128)} fusion(f32[1024,2048]{1,0:T(8,128)} %squeeze.24, f32[1024,2048]{1,0:T(8,128)} %squeeze.25), kind=kLoop, calls=%fused_computation.5 | loop fusion | flops 4194304 | bytes 25165824 | tf_op jit(solution)/shard_map/sub | solution.py:100
  422.2 17.0 %convolution_bitcast_fusion.1 = f32[512,1024]{0,1:T(8,128)} fusion(f32[1024,2048]{1,0:T(8,128)} %squeeze.25, f32[2048,512]{1,0:T(8,128)} %param.13), kind=kOutput, calls=%fused_computation.48 | convolution fusion | flops 12884901888 | bytes 14680064 | tf_op jit(solution)/shard_map/dot_general | solution.py:130
  441.3 34.1 %all-gather.9.cloned.1.call-done = f32[32,1,8192]{2,1,0:T(1,128)} async-done(((f32[1,1,8192]{2,1,0:T(1,128)}), f32[32,1,8192]{2,1,0:T(1,128)}) %all-gather.9.cloned.1.call-update) | async-done | bytes 1048592 | tf_op jit(solution)/shard_map/all_gather | solution.py:115
  492.6 11.7 %cholesky.104 = f32[128,128]{1,0:T(8,128)S(1)} custom-call(f32[128,128]{1,0:T(8,128)S(1)} %cholesky.266), custom_call_target="Cholesky" | custom-call | tf_op jit(solution)/shard_map/jit(cholesky)/cholesky | solution.py:125
  504.5 9.8 %custom-call.34 = f32[1,128,128]{1,2,0:T(8,128)S(1)} custom-call(f32[1,128,128]{2,1,0:T(8,128)S(1)} %get-tuple-element.55), custom_call_target="InvertDiagBlocksLowerTriangular" | custom-call | tf_op jit(solution)/shard_map/jit(cholesky)/cholesky | solution.py:125
  515.0 11.7 %cholesky.217 = f32[128,128]{1,0:T(8,128)S(1)} custom-call(f32[128,128]{1,0:T(8,128)S(1)} %cholesky.270), custom_call_target="Cholesky" | custom-call | tf_op jit(solution)/shard_map/jit(cholesky)/cholesky | solution.py:125
  526.7 10.0 %custom-call.35 = f32[1,128,128]{1,2,0:T(8,128)S(1)} custom-call(f32[1,128,128]{2,1,0:T(8,128)S(1)} %get-tuple-element.52), custom_call_target="InvertDiagBlocksLowerTriangular" | custom-call | tf_op jit(solution)/shard_map/jit(cholesky)/cholesky | solution.py:125
  537.4 11.7 %cholesky.238 = f32[128,128]{1,0:T(8,128)S(1)} custom-call(f32[128,128]{1,0:T(8,128)S(1)} %cholesky.275), custom_call_target="Cholesky" | custom-call | tf_op jit(solution)/shard_map/jit(cholesky)/cholesky | solution.py:125
  549.1 9.8 %custom-call.36 = f32[1,128,128]{1,2,0:T(8,128)S(1)} custom-call(f32[1,128,128]{2,1,0:T(8,128)S(1)} %get-tuple-element.49), custom_call_target="InvertDiagBlocksLowerTriangular" | custom-call | tf_op jit(solution)/shard_map/jit(cholesky)/cholesky | solution.py:125
  559.5 11.7 %cholesky.255 = f32[128,128]{1,0:T(8,128)S(1)} custom-call(f32[128,128]{1,0:T(8,128)S(1)} %convolution_subtract_fusion.10), custom_call_target="Cholesky" | custom-call | tf_op jit(solution)/shard_map/jit(cholesky)/cholesky | solution.py:125
  576.5 10.6 %while.1 = (s32[]{:T(128)}, f32[512,512]{1,0:T(8,128)S(1)}, s32[4,2]{0,1:T(2,128)S(1)}, f32[4,128,128]{2,1,0:T(8,128)}, s32[]{:T(128)}) while((s32[]{:T(128)}, f32[512,512]{1,0:T(8,128)S(1)}, s32[4,2]{0,1:T(2,128)S(1)}, f32[4,128,128]{2,1,0:T(8,128)}, s32[]{:T(128)}) %tuple.52), condition=%wide.while_cond, body=%wide.while_body.sunk | while | flops 2 | bytes 132705 | solution.py:16
  587.2 40.2 %custom-call.37 = f32[4,128,128]{1,2,0:T(8,128)S(1)} custom-call(f32[4,128,128]{2,1,0:T(8,128)} %get-tuple-element.9), custom_call_target="InvertDiagBlocksLowerTriangular" | custom-call | tf_op jit(solution)/shard_map/triangular_solve | solution.py:16
  641.1 14.3 %all_gather.15 = f32[128,512]{0,1:T(8,128)S(1)} all-gather(f32[128,64]{0,1:T(8,128)S(1)} %slice.193), channel_id=1, replica_groups=mesh['row'=8,'col'=4] {'row'}, dimensions={1}, use_global_device_ids=true | all-gather | bytes 294912 | tf_op jit(solution)/shard_map/all_gather | solution.py:135
  678.0 16.4 %fusion.18 = f32[1024,2048]{1,0:T(8,128)} fusion(f32[1024,2048]{1,0:T(8,128)S(1)} %bitcast.163, f32[128,2048]{1,0:T(8,128)S(1)} %fusion.102, f32[128,2048]{1,0:T(8,128)S(1)} %fusion.99, f32[128,2048]{1,0:T(8,128)S(1)} %fusion.96, f32[128,2048]{1,0:T(8,128)S(1)} %fusion.50, f32[128,1024]{1,0:T(8,128)S(1)} %copy-done.14, f32[128,1024]{1,0:T(8,128)S(1)} %copy-done.11, ...), kind=kOutput, calls=%fused_computation.28 | convolution fusion | flops 12891717632 | bytes 23068672 | tf_op jit(solution)/shard_map/dot_general | solution.py:24
  (145 shorter events, 102.1 us)
Async XLA Ops:
  7.2 2.0 copy-start
  9.2 14.3 %copy-start.16 = (f32[1,1024,1024]{2,1,0:T(8,128)S(1)}, f32[1,1024,1024]{2,1,0:T(8,128)}, u32[]{:S(2)}) copy-start(f32[1,1024,1024]{2,1,0:T(8,128)} %param.7) | copy-start | bytes 12582916
  21.8 1.7 copy-start.4
  23.4 12.1 %copy-start.15 = (f32[1,768]{1,0:T(1,128)S(1)}, f32[1,768]{1,0:T(1,128)}, u32[]{:S(2)}) copy-start(f32[1,768]{1,0:T(1,128)} %param.11) | copy-start | bytes 9220
  23.4 12.2 %copy-start.17 = (f32[1,1024]{1,0:T(1,128)S(1)}, f32[1,1024]{1,0:T(1,128)}, u32[]{:S(2)}) copy-start(f32[1,1024]{1,0:T(1,128)} %param.10) | copy-start | bytes 12292
  60.4 8.4 %copy-start.5 = (f32[1024,768]{1,0:T(8,128)S(1)}, f32[1024,768]{1,0:T(8,128)}, u32[]{:S(2)}) copy-start(f32[1024,768]{1,0:T(8,128)} %copy-done.4) | copy-start | bytes 9437188
  95.7 8.5 %copy-start.12 = (f32[576,1,1024]{2,0,1:T(8,128)S(1)}, f32[576,1,1024]{2,0,1:T(8,128)}, u32[]{:S(2)}) copy-start(f32[576,1,1024]{2,0,1:T(8,128)} %stack_reshape.7) | copy-start | bytes 7077892
  117.7 113.3 %all-to-all-start = ((f32[32,18,2,1024]{3,2,1,0:T(2,128)}), f32[32,18,2,1024]{3,2,1,0:T(2,128)}, u32[]{:S(2)}, u32[]{:S(2)}) async-start(f32[32,18,2,1024]{3,2,1,0:T(2,128)} %copy.109), calls=%async_computation | async-start | bytes 9437184 | tf_op jit(solution)/shard_map/all_to_all | solution.py:83
  125.2 350.1 %all-gather.9.cloned.1.call-start = ((), (), s32[]{:S(2)}) async-start(), calls=%async_computation.5 | async-start | bytes 1081344 | tf_op jit(solution)/shard_map/all_gather | solution.py:115
  420.2 207.1 %all-gather.5.cloned.1.call-start = ((), (), s32[]{:S(2)}) async-start(), calls=%async_computation.2 | async-start | bytes 2621440 | tf_op jit(solution)/shard_map/all_gather | solution.py:103
  422.2 218.1 %reduce-scatter.2.cloned.1.call-start = ((), (), s32[]{:S(2)}) async-start(), calls=%async_computation.4 | async-start | bytes 2621440 | tf_op jit(solution)/shard_map/reduce_scatter | solution.py:129
  439.3 227.4 %all-gather.7.cloned.1.call-start = ((), (), s32[]{:S(2)}) async-start(), calls=%async_computation.3 | async-start | bytes 4718592 | tf_op jit(solution)/shard_map/all_gather | solution.py:109
  587.2 43.1 %copy-start.8 = (f32[512,512]{1,0:T(8,128)}, f32[512,512]{1,0:T(8,128)S(1)}, u32[]{:S(2)}) copy-start(f32[512,512]{1,0:T(8,128)S(1)} %get-tuple-element.117) | copy-start | bytes 3145732
  632.8 26.4 %copy-start.2 = (f32[128,1024]{1,0:T(8,128)}, f32[128,1024]{1,0:T(8,128)S(1)}, u32[]{:S(2)}) copy-start(f32[128,1024]{1,0:T(8,128)S(1)} %fusion.58) | copy-start | bytes 1572868
  634.9 24.3 %copy-start.6 = (f32[128,1024]{1,0:T(8,128)}, f32[128,1024]{1,0:T(8,128)S(1)}, u32[]{:S(2)}) copy-start(f32[128,1024]{1,0:T(8,128)S(1)} %fusion.97) | copy-start | bytes 1572868
  637.3 2.2 copy-start.10
  639.6 19.0 %copy-start.9 = (f32[512,512]{1,0:T(8,128)S(1)}, f32[512,512]{1,0:T(8,128)}, u32[]{:S(2)}) copy-start(f32[512,512]{1,0:T(8,128)} %copy-done.8) | copy-start | bytes 3145732
  640.2 24.4 %copy-start.13 = (f32[128,1024]{1,0:T(8,128)}, f32[128,1024]{1,0:T(8,128)S(1)}, u32[]{:S(2)}) copy-start(f32[128,1024]{1,0:T(8,128)S(1)} %fusion.103) | copy-start | bytes 1572868
  671.2 6.7 slice-start
  673.5 4.4 slice-start.1
  674.6 3.4 copy-start.3
  674.6 3.4 copy-start.7
  674.6 3.4 copy-start.11
  674.6 3.4 copy-start.14
  678.0 16.4 %copy-start.1 = (f32[1,1024,768]{2,1,0:T(8,128)S(1)}, f32[1,1024,768]{2,1,0:T(8,128)}, u32[]{:S(2)}) copy-start(f32[1,1024,768]{2,1,0:T(8,128)} %param.8) | copy-start | bytes 9437188
Sparse Core Ops, SparseCore 0:
  420.3 54.9 all-gather.8
  477.7 34.0 all-gather.4
  514.8 35.3 reduce-scatter.1
  551.6 46.9 all-gather.6
where the time goes:
time: 709 us; the launch traced here: 701 us
  local copies, waits for them, and re-layouts  226 us (32%)
  matrix products  160 us (23%)
  waiting for transfers between devices  139 us (20%)
  other arithmetic  137 us (19%)
  between operations  17.2 us (2%)
  blocking collectives  14.3 us (2%)
  starting transfers between devices  7.61 us (1%)
    all_to_all x1, waiting for transfers between devices, body(): lax.all_to_all(outbox, ('row', 'col'), split_axis=0, concat_axis=0, tiled...  105 us
    another operation x15, other arithmetic, body(): lower = jnp.linalg.cholesky(corner)  79.2 us
    dot_general x3, matrix products, matmul(): return jnp.dot(left, right, precision=highest)  64.9 us
    dot_general x5, matrix products, tmatmul(): lax.dot_general(left, right, (((0,), (0,)), ((), ())), precision=highest)  55.9 us
    slice x2, local copies, waits for them, and re-layouts, body(): mass_local = local[1]  44.3 us
    another operation x3, other arithmetic, lower_solve(): return lax.linalg.triangular_solve(lower, rhs, left_side=True, lower=True)  40.3 us
    all_gather x1, waiting for transfers between devices, body(): lax.all_gather(shifted[:panel_row_count, :panel_col_count].reshape(1, pan...  34.1 us
    reshape x4, local copies, waits for them, and re-layouts, to_tiles(): matrix.reshape(blocks_per_side, SUB, blocks_per_side, SUB)  29.8 us
  transfers between devices with their start and end apart: 5, of which 2 were waited for; matrix products, arithmetic and copies ran while one was open for 28% of the time, Pallas kernels for 0%

commit v1 on v0

v1 whole, which is shorter than its diff:
```python
import functools
import jax
import jax.numpy as jnp
from jax import lax
from jax.experimental import pallas as pl
from jax.experimental.pallas import tpu as pltpu
from jax.sharding import PartitionSpec as P

IDB = 128
SUB = 32
NG = 8192
PANEL = 512
PER_RUN = IDB // SUB
LANES = 128
SUBLANES = 8
GROUPS = SUB // SUBLANES

highest = lax.Precision.HIGHEST
high = lax.Precision.HIGH
shift_value = 0.05
VMEM_LIMIT = 60 * 1024 * 1024


def tdot(left, right, precision):
    return lax.dot_general(left, right, (((0,), (0,)), ((), ())), precision=precision)


class Grid:
    def __init__(self, row_count, col_count):
        self.rows = row_count
        self.cols = col_count
        self.devices = row_count * col_count
        self.row_classes = row_count // PER_RUN
        self.col_classes = col_count // PER_RUN
        self.row_cap = 3
        self.col_cap = 3 + (self.row_classes // self.col_classes - 1) * (3 // (self.row_classes - 1))
        self.slots = self.row_cap * self.col_cap


def call(kernel, out_shape, in_specs, scratch=(), flops=0, nbytes=0):
    return pl.pallas_call(
        kernel,
        out_shape=out_shape,
        in_specs=in_specs,
        out_specs=jax.tree.map(lambda _: pl.BlockSpec(memory_space=pltpu.VMEM), out_shape),
        scratch_shapes=list(scratch),
        compiler_params=pltpu.CompilerParams(vmem_limit_bytes=VMEM_LIMIT),
        cost_estimate=pl.CostEstimate(flops=flops, bytes_accessed=nbytes, transcendentals=0),
    )


SMEM = pl.BlockSpec(memory_space=pltpu.SMEM)
VMEM = pl.BlockSpec(memory_space=pltpu.VMEM)


def ranks_of(groups, classes):
    kinds = [g % classes for g in groups]
    ranks = []
    for j in range(len(kinds)):
        rank = jnp.int32(0)
        for i in range(j):
            rank = rank + jnp.where(kinds[i] == kinds[j], 1, 0).astype(jnp.int32)
        ranks.append(rank)
    return kinds, ranks


def lane_group():
    return lax.broadcasted_iota(jnp.int32, (SUBLANES, LANES), 1) // SUB


def regroup(tile):
    parts = [tile[SUBLANES * q : SUBLANES * (q + 1)] for q in range(GROUPS)]
    where = lane_group()
    out = []
    for k in range(PER_RUN):
        value = None
        for q in range(GROUPS):
            turn = (q - k) % PER_RUN * SUB
            piece = parts[q] if turn == 0 else pltpu.roll(parts[q], turn, 1)
            value = piece if value is None else jnp.where(where == q, piece, value)
        out.append(value)
    return out


def pack_matrix(grid, runs_ref, own_ref, a_ref, out_ref):
    number = a_ref.shape[0] // IDB
    groups = [runs_ref[own_ref[0], j] for j in range(number)]
    row_kind, row_rank = ranks_of(groups, grid.row_classes)
    col_kind, col_rank = ranks_of(groups, grid.col_classes)
    if grid.devices * grid.slots != (number * PER_RUN) ** 2:
        out_ref[...] = jnp.zeros_like(out_ref)
    for i in range(number):
        for k in range(PER_RUN):
            for j in range(number):
                tile = a_ref[i * IDB + k * SUB : i * IDB + (k + 1) * SUB, j * IDB : (j + 1) * IDB]
                row = (row_kind[i] * PER_RUN + k) * grid.cols
                slot = row_rank[i] * grid.col_cap + col_rank[j]
                for kk, value in enumerate(regroup(tile)):
                    out_ref[row + col_kind[j] * PER_RUN + kk, slot] = value


def pack_modes(grid, per_device, runs_ref, own_ref, y_ref, out_ref):
    number = y_ref.shape[1] // IDB
    groups = [runs_ref[own_ref[0], j] for j in range(number)]
    row_kind, row_rank = ranks_of(groups, grid.row_classes)
    if grid.devices * grid.row_cap != number * PER_RUN * grid.cols:
        out_ref[...] = jnp.zeros_like(out_ref)
    for m in range(y_ref.shape[0] // SUB):
        for j in range(number):
            tile = y_ref[m * SUB : (m + 1) * SUB, j * IDB : (j + 1) * IDB]
            slot = row_rank[j] * per_device + m % per_device
            for k, value in enumerate(regroup(tile)):
                row = (row_kind[j] * PER_RUN + k) * grid.cols + m // per_device
                out_ref[row, slot] = value


def list_places(runs_ref, source, number, classes, kind, cap, table_ref):
    count = jnp.int32(0)
    for j in range(number):
        g = runs_ref[source, j]
        table_ref[source, count] = g // classes
        count = count + jnp.where(g % classes == kind, 1, 0).astype(jnp.int32)
    for t in range(cap):
        table_ref[source, t] = jnp.where(t < count, table_ref[source, t], -1)


def add_block(acc_ref, row, place, value):
    valid = place >= 0
    place = jnp.maximum(place, 0)
    turn = place % PER_RUN
    start = pl.multiple_of(place // PER_RUN * LANES, LANES)
    mask = (lane_group() == turn) & valid
    parts = []
    for q in range(GROUPS):
        moved = pltpu.roll(value, (turn - q + PER_RUN) % PER_RUN * SUB, 1)
        parts.append(jnp.where(mask, moved, 0.0))
    acc_ref[pl.ds(row, SUB), pl.ds(start, LANES)] += jnp.concatenate(parts, axis=0)


def place_matrix(grid, runs_ref, own_ref, in_ref, acc_ref, row_tab, col_tab):
    sources, number = runs_ref.shape
    row_kind = own_ref[0] // grid.cols // PER_RUN
    col_kind = own_ref[0] % grid.cols // PER_RUN
    acc_ref[...] = jnp.zeros_like(acc_ref)

    @pl.loop(0, sources)
    def _(s):
        list_places(runs_ref, s, number, grid.row_classes, row_kind, grid.row_cap, row_tab)
        list_places(runs_ref, s, number, grid.col_classes, col_kind, grid.col_cap, col_tab)

    @pl.loop(0, sources)
    def _(s):
        for t in range(grid.row_cap):
            row_place = row_tab[s, t]
            row = pl.multiple_of(jnp.maximum(row_place, 0) * SUB, SUB)
            for u in range(grid.col_cap):
                place = jnp.where(row_place >= 0, col_tab[s, u], -1)
                add_block(acc_ref, row, place, in_ref[s, t * grid.col_cap + u])


def place_modes(grid, per_device, runs_ref, own_ref, in_ref, acc_ref, row_tab):
    sources, number = runs_ref.shape
    row_kind = own_ref[0] // grid.cols // PER_RUN
    acc_ref[...] = jnp.zeros_like(acc_ref)

    @pl.loop(0, sources)
    def _(s):
        list_places(runs_ref, s, number, grid.row_classes, row_kind, grid.row_cap, row_tab)

    @pl.loop(0, sources)
    def _(s):
        for t in range(grid.row_cap):
            place = row_tab[s, t]
            for m in range(per_device):
                add_block(acc_ref, m * SUB, place, in_ref[s, t * per_device + m])


def pick_modes(grid, runs_ref, own_ref, modes_ref, out_ref):
    number = runs_ref.shape[1]
    own_row = own_ref[0] // grid.cols
    col_kind = own_ref[0] % grid.cols // PER_RUN
    if grid.cols * grid.col_cap != number * PER_RUN:
        out_ref[...] = jnp.zeros_like(out_ref)
    for c in range(grid.cols):
        groups = [runs_ref[own_row * grid.cols + c, j] for j in range(number)]
        kinds, ranks = ranks_of(groups, grid.col_classes)
        for j in range(number):

            @pl.when(kinds[j] == col_kind)
            def _():
                row = pl.multiple_of(groups[j] // grid.col_classes * SUB, SUB)
                out_ref[c, ranks[j]] = modes_ref[pl.ds(row, SUB), :]


def order_modes(grid, runs_ref, own_ref, in_ref, out_ref):
    number = runs_ref.shape[1]
    groups = [runs_ref[own_ref[0], j] for j in range(number)]
    kinds, ranks = ranks_of(groups, grid.col_classes)
    for j in range(number):
        for k in range(PER_RUN):
            start = j * IDB + k * SUB
            out_ref[start : start + SUB, :] = in_ref[kinds[j] * PER_RUN + k, ranks[j]]


def invert_block(matrix):
    n = matrix.shape[0]
    count = n // SUBLANES
    sub = lax.broadcasted_iota(jnp.int32, (SUBLANES, n), 0)
    lane = lax.broadcasted_iota(jnp.int32, (SUBLANES, n), 1)

    def across(value, m):
        return jnp.broadcast_to(value[:, m : m + 1], (SUBLANES, n))

    def down(value, k):
        return jnp.broadcast_to(value[k : k + 1, :], (SUBLANES, n))

    def panel(_, rows):
        head = rows[0]
        split = [across(head, m) for m in range(SUBLANES)]
        for k in range(SUBLANES):
            inverse = 1.0 / down(split[k], k)
            mine = sub == k
            head = jnp.where(lane == k, jnp.where(mine, 1.0, 0.0), head)
            pivot = down(head, k) * inverse
            factor = split[k]
            head = jnp.where(mine, pivot, head - factor * pivot)
            for m in range(k + 1, SUBLANES):
                scaled = down(split[m], k) * inverse
                split[m] = jnp.where(mine, scaled, split[m] - factor * scaled)
        lines = [down(head, m) for m in range(SUBLANES)]
        done = []
        for row in rows[1:]:
            value = jnp.where(lane < SUBLANES, 0.0, row)
            for m in range(SUBLANES):
                value = value - across(row, m) * lines[m]
            done.append(value)
        done.append(head)
        return tuple(pltpu.roll(value, n - SUBLANES, 1) for value in done)

    rows = tuple(matrix[SUBLANES * i : SUBLANES * (i + 1)] for i in range(count))
    rows = lax.fori_loop(0, count, panel, rows)
    return jnp.concatenate(rows, axis=0)


def invert_corner(grid, pieces_ref, out_ref, work_ref):
    row_blocks = PANEL // SUB // grid.rows
    col_blocks = PANEL // SUB // grid.cols
    width = col_blocks * SUB

    def col_position(block):
        return (block % grid.cols) * col_blocks + block // grid.cols

    for r in range(grid.rows):
        for b in range(row_blocks):
            start = col_position(r + grid.rows * b) * SUB
            for c in range(grid.cols):
                work_ref[start : start + SUB, c * width : (c + 1) * width] = pieces_ref[
                    r * grid.cols + c, b * SUB : (b + 1) * SUB, :
                ]
    steps = PANEL // LANES
    lane = lax.broadcasted_iota(jnp.int32, (LANES, PANEL), 1) // LANES

    @pl.loop(0, steps)
    def _(step):
        at = pl.ds(pl.multiple_of(step * LANES, LANES), LANES)
        small = invert_block(work_ref[at, at])
        line = jnp.dot(small, work_ref[at, :], precision=highest, preferred_element_type=jnp.float32)
        line = jnp.where(lane == step, jnp.concatenate([small] * steps, axis=1), line)
        for i in range(steps):
            rows = slice(i * LANES, (i + 1) * LANES)
            factor = work_ref[rows, at]
            kept = jnp.where(lane == step, 0.0, work_ref[rows, :])
            update = kept - jnp.dot(
                factor, line, precision=highest, preferred_element_type=jnp.float32
            )
            work_ref[rows, :] = jnp.where(i == step, line, update)

    for r in range(grid.rows):
        for b in range(row_blocks):
            source = col_position(r + grid.rows * b) * SUB
            target = (r * row_blocks + b) * SUB
            out_ref[target : target + SUB, :] = work_ref[source : source + SUB, :]


def spread(value, axis, count):
    copies = jnp.broadcast_to(value[None], (count,) + value.shape)
    return lax.all_to_all(copies, axis, 0, 0, tiled=True)


def body(
    inverse_factor,
    coupling,
    boundary_stiffness,
    interior_mass,
    boundary_mass,
    interface_ids,
    trial_modes,
):
    grid = Grid(lax.axis_size("row"), lax.axis_size("col"))
    f32 = jnp.float32
    modes = trial_modes.shape[1]
    mode_count = modes // grid.cols
    per_device = mode_count // SUB
    size = coupling.shape[2]
    sources = interface_ids.shape[0]
    local_rows = NG // grid.rows
    local_cols = NG // grid.cols
    runs = interface_ids[:, ::IDB] // IDB
    own = (lax.axis_index("row") * grid.cols + lax.axis_index("col")).astype(jnp.int32).reshape(1)

    wanted = call(
        functools.partial(pick_modes, grid),
        jax.ShapeDtypeStruct((grid.cols, grid.col_cap, SUB, modes), f32),
        [SMEM, SMEM, VMEM],
        nbytes=trial_modes.size * 8,
    )(runs, own, trial_modes)
    wanted = lax.all_to_all(wanted, "col", 0, 0, tiled=True)

    factor = inverse_factor[0]
    weighted = jnp.dot(factor, coupling[0], precision=high)
    static = tdot(factor, weighted, high)
    condensed_m = jnp.diag(boundary_mass[0]) + tdot(static, interior_mass[0][:, None] * static, high)
    shifted_s = boundary_stiffness[0] - tdot(weighted, weighted, high) - shift_value * condensed_m

    outbox = call(
        functools.partial(pack_matrix, grid),
        jax.ShapeDtypeStruct((grid.devices, grid.slots, SUBLANES, LANES), f32),
        [SMEM, SMEM, VMEM],
        nbytes=size * size * 8,
    )(runs, own, shifted_s)
    inbox = lax.all_to_all(outbox, ("row", "col"), 0, 0, tiled=True)

    own_modes = call(
        functools.partial(order_modes, grid),
        jax.ShapeDtypeStruct((size, modes), f32),
        [SMEM, SMEM, VMEM],
        nbytes=size * modes * 8,
    )(runs, own, wanted)
    weighted_modes = tdot(own_modes, condensed_m, high)
    mode_outbox = call(
        functools.partial(pack_modes, grid, per_device),
        jax.ShapeDtypeStruct((grid.devices, grid.row_cap * per_device, SUBLANES, LANES), f32),
        [SMEM, SMEM, VMEM],
        nbytes=size * modes * 8,
    )(runs, own, weighted_modes)
    mode_outbox, inbox = lax.optimization_barrier((mode_outbox, inbox))
    mode_inbox = lax.all_to_all(mode_outbox, ("row", "col"), 0, 0, tiled=True)

    shifted = call(
        functools.partial(place_matrix, grid),
        jax.ShapeDtypeStruct((local_rows, local_cols), f32),
        [SMEM, SMEM, VMEM],
        [
            pltpu.SMEM((sources, size // IDB + 1), jnp.int32),
            pltpu.SMEM((sources, size // IDB + 1), jnp.int32),
        ],
        nbytes=local_rows * local_cols * 8,
    )(runs, own, inbox)

    panel_row_count = PANEL // grid.rows
    panel_col_count = PANEL // grid.cols
    pieces = spread(shifted[:panel_row_count, :panel_col_count], ("row", "col"), grid.devices)
    panel_cols = spread(shifted[:, :panel_col_count], "col", grid.cols)
    panel_cols = panel_cols.transpose(1, 0, 2).reshape(local_rows, PANEL)
    panel_rows = lax.all_gather(shifted[:panel_row_count, :], "row", axis=0, tiled=True)

    inverse = call(
        functools.partial(invert_corner, grid),
        jax.ShapeDtypeStruct((PANEL, PANEL), f32),
        [VMEM],
        [pltpu.VMEM((PANEL, PANEL), f32)],
        flops=4 * PANEL**3,
        nbytes=PANEL * PANEL * 80,
    )(pieces)

    solved = lax.dot_general(inverse, panel_cols, (((1,), (1,)), ((), ())), precision=highest)
    reduced_matrix = shifted - tdot(solved, panel_rows, high)

    modes_local = call(
        functools.partial(place_modes, grid, per_device),
        jax.ShapeDtypeStruct((mode_count, local_rows), f32),
        [SMEM, SMEM, VMEM],
        [pltpu.SMEM((sources, size // IDB + 1), jnp.int32)],
        nbytes=mode_count * local_rows * 8,
    )(runs, own, mode_inbox)
    panel_modes = spread(modes_local[:, :panel_row_count].T, "row", grid.rows).reshape(PANEL, -1)
    reduced_columns = modes_local - tdot(panel_modes, solved, high)
    return (reduced_matrix, reduced_columns)


def solution(mesh):
    return jax.shard_map(
        body,
        mesh=mesh,
        in_specs=(
            P(("row", "col"), None, None),
            P(("row", "col"), None, None),
            P(("row", "col"), None, None),
            P(("row", "col"), None),
            P(("row", "col"), None),
            P(),
            P("col", None),
        ),
        out_specs=(P("row", "col"), P("col", "row")),
        check_vma=False,
    )
```

time: 709 us -> 320 us (0.45); the launches traced: 701 us -> 319 us
  local copies, waits for them, and re-layouts: 226 us -> 12.4 us
  other arithmetic: 137 us -> 0.63 us
  matrix products: 160 us -> 53.3 us
  Pallas kernels: 0 us -> 76.6 us
  starting transfers between devices: 7.61 us -> 26.9 us
  blocking collectives: 14.3 us -> 0 us
    another operation x18 -> x0, other arithmetic: 120 us -> none  [the longest x15 79.2 us: body(): lower = jnp.linalg.cholesky(corner)]
    dot_general x9 -> x8, matrix products: 138 us -> 53.3 us  [the longest x6 40.3 us: tdot(): lax.dot_general(left, right, (((0,), (0,)), ((), ())), precision=precision)]
    pallas_call x0 -> x7, Pallas kernels: none -> 76.6 us  [the longest x1 33.5 us: body(): call(functools.partial(invert_corner, grid), jax.ShapeDtypeStruct((PANEL,...]
    slice x6 -> x3, local copies, waits for them, and re-layouts: 71.2 us -> 2.4 us  [the longest x2 1.27 us: body(): panel_cols = spread(shifted[:, :panel_col_count], 'col', grid.cols)]
    squeeze x2 -> x0, local copies, waits for them, and re-layouts: 51.1 us -> none  [the longest x1 25.7 us: body(): mass_local = local[1]]
    reshape x9 -> x0, local copies, waits for them, and re-layouts: 39.9 us -> none  [the longest x4 29.8 us: to_tiles(): matrix.reshape(blocks_per_side, SUB, blocks_per_side, SUB)]
    all_gather x2 -> x0, waiting for transfers between devices: 34.1 us -> none  [the longest x1 34.1 us: body(): lax.all_gather(shifted[:panel_row_count, :panel_col_count].reshape(1, pan...]
    all_to_all x1 -> x6, waiting for transfers between devices: 105 us -> 135 us  [the longest x1 52.4 us: body(): mode_inbox = lax.all_to_all(mode_outbox, ('row', 'col'), 0, 0, tiled=True)]
  transfers between devices with their start and end apart: 5 -> 7, of which waited for: 2 -> 4; matrix products, arithmetic and copies ran while one was open for 28% -> 14% of each run, Pallas kernels for 0% -> 17%
where the time goes in v1:
time: 320 us; the launch traced here: 319 us
  waiting for transfers between devices  135 us (42%)
  Pallas kernels  76.6 us (24%)
  matrix products  53.3 us (17%)
  starting transfers between devices  26.9 us (8%)
  between operations  14.2 us (4%)
  local copies, waits for them, and re-layouts  12.4 us (4%)
    all_to_all x1, waiting for transfers between devices, body(): mode_inbox = lax.all_to_all(mode_outbox, ('row', 'col'), 0, 0, tiled=True)  52.4 us
    all_to_all x1, waiting for transfers between devices, body(): inbox = lax.all_to_all(outbox, ('row', 'col'), 0, 0, tiled=True)  42.9 us
    dot_general x6, matrix products, tdot(): lax.dot_general(left, right, (((0,), (0,)), ((), ())), precision=precision)  40.3 us
    all_to_all x3, waiting for transfers between devices, spread(): return lax.all_to_all(copies, axis, 0, 0, tiled=True)  40 us
    pallas_call x1, Pallas kernels, body(): call(functools.partial(invert_corner, grid), jax.ShapeDtypeStruct((PANEL,...  33.5 us
    pallas_call x1, Pallas kernels, body(): call(functools.partial(place_matrix, grid), jax.ShapeDtypeStruct((local_r...  19.7 us
    all_to_all x3, starting transfers between devices, spread(): return lax.all_to_all(copies, axis, 0, 0, tiled=True)  10.7 us
    pallas_call x1, Pallas kernels, body(): call(functools.partial(place_modes, grid, per_device), jax.ShapeDtypeStru...  8.43 us
  transfers between devices with their start and end apart: 7, of which 4 were waited for; matrix products, arithmetic and copies ran while one was open for 14% of the time, Pallas kernels for 17%

profile of v1, /device:TPU:0, one launch (start us, length us, event | category | flops | bytes accessed | tf_op | source)
XLA Modules:
  0.0 319.4 jit_solution(16708117269959748278)
XLA Ops:
  7.2 1.1 slice.15
  8.9 3.5 %shard_map.86 = f32[4,6,32,512]{3,2,1,0:T(8,128)} custom-call(s32[32,6]{1,0:T(8,128)} %add_select_fusion.runs_ref, s32[1]{0:T(128)} %bitcast.own_ref, f32[2048,512]{1,0:T(8,128)} %modes_ref.1), custom_call_target="tpu_custom_call" | custom-call | bytes 8388608 | tf_op jit(solution)/shard_map/pallas_call | solution.py:311
  12.4 5.2 %all-to-all-start = ((f32[4,6,32,512]{3,2,1,0:T(8,128)}), f32[4,6,32,512]{3,2,1,0:T(8,128)}, u32[]{:S(2)}, u32[]{:S(2)}) async-start(f32[4,6,32,512]{3,2,1,0:T(8,128)} %shard_map.86), calls=%async_computation | async-start | bytes 3145728 | tf_op jit(solution)/shard_map/all_to_all | solution.py:317
  17.6 7.5 %fusion.4 = f32[1024,768]{1,0:T(8,128)S(1)} fusion(f32[1,1024,1024]{2,1,0:T(8,128)} %param.7, f32[1,1024,768]{2,1,0:T(8,128)S(1)} %copy-done), kind=kOutput, calls=%fused_computation.4 | convolution fusion | flops 4831838208 | bytes 10485760 | tf_op jit(solution)/shard_map/dot_general | solution.py:320
  25.2 1.6 copy-done.3
  26.8 6.9 %fusion.2 = f32[768,1024]{1,0:T(8,128)} fusion(f32[1024,768]{1,0:T(8,128)S(1)} %fusion.4, f32[1,1024,1024]{2,1,0:T(8,128)S(1)} %copy-done.11), kind=kOutput, calls=%fused_computation.2 | convolution fusion | flops 4831838208 | bytes 10485760 | tf_op jit(solution)/shard_map/dot_general | solution.py:25
  33.8 6.9 %fusion = f32[768,768]{1,0:T(8,128)S(1)} fusion(f32[768,1024]{1,0:T(8,128)} %fusion.2, f32[1024]{0:T(1024)S(1)} %bitcast.33), kind=kOutput, calls=%fused_computation | convolution fusion | flops 3624665088 | bytes 5509120 | tf_op jit(solution)/shard_map/dot_general | solution.py:25
  40.8 6.8 %fusion.7.a_ref = f32[768,768]{1,0:T(8,128)} fusion(f32[1,768,768]{2,1,0:T(8,128)S(1)} %copy-done.8, f32[768,768]{1,0:T(8,128)S(1)} %fusion, f32[1024,768]{1,0:T(8,128)S(1)} %copy-done.4, f32[768]{0:T(1024)S(1)} %reduce), kind=kOutput, calls=%fused_computation.9 | convolution fusion | flops 3627417600 | bytes 10226688 | tf_op jit(solution)/shard_map/dot_general | solution.py:25
  47.5 5.0 %shard_map.89 = f32[32,18,8,128]{3,2,1,0:T(8,128)} custom-call(s32[32,6]{1,0:T(8,128)} %add_select_fusion.runs_ref, s32[1]{0:T(128)} %bitcast.own_ref, f32[768,768]{1,0:T(8,128)} %fusion.7.a_ref), custom_call_target="tpu_custom_call" | custom-call | bytes 4718592 | tf_op jit(solution)/shard_map/pallas_call | solution.py:325
  52.5 7.0 %all-to-all-start.1 = ((f32[32,18,8,128]{3,2,1,0:T(8,128)}), f32[32,18,8,128]{3,2,1,0:T(8,128)}, u32[]{:S(2)}, u32[]{:S(2)}) async-start(f32[32,18,8,128]{3,2,1,0:T(8,128)} %shard_map.89), calls=%async_computation.1 | async-start | bytes 4718592 | tf_op jit(solution)/shard_map/all_to_all | solution.py:331
  59.6 2.7 shard_map.87
  62.2 4.9 %fusion.8.y_ref = f32[512,768]{1,0:T(8,128)} fusion(f32[768,512]{1,0:T(8,128)} %shard_map.87, f32[768,768]{1,0:T(8,128)S(1)} %fusion, f32[768]{0:T(1024)S(1)} %reduce), kind=kOutput, calls=%fused_computation.12 | convolution fusion | flops 1813708800 | bytes 5508096 | tf_op jit(solution)/shard_map/dot_general | solution.py:25
  67.2 3.8 %shard_map.88 = f32[32,12,8,128]{3,2,1,0:T(8,128)} custom-call(s32[32,6]{1,0:T(8,128)} %add_select_fusion.runs_ref, s32[1]{0:T(128)} %bitcast.own_ref, f32[512,768]{1,0:T(8,128)} %fusion.8.y_ref), custom_call_target="tpu_custom_call" | custom-call | bytes 3145728 | tf_op jit(solution)/shard_map/pallas_call | solution.py:340
  71.0 42.9 %all-to-all-done.1.in_ref = f32[32,18,8,128]{3,2,1,0:T(8,128)} async-done(((f32[32,18,8,128]{3,2,1,0:T(8,128)}), f32[32,18,8,128]{3,2,1,0:T(8,128)}, u32[]{:S(2)}, u32[]{:S(2)}) %all-to-all-start.1) | async-done | bytes 2359328 | tf_op jit(solution)/shard_map/all_to_all | solution.py:331
  113.8 19.7 %shard_map.90 = f32[1024,2048]{1,0:T(8,128)} custom-call(s32[32,6]{1,0:T(8,128)} %add_select_fusion.runs_ref, s32[1]{0:T(128)} %bitcast.own_ref, f32[32,18,8,128]{3,2,1,0:T(8,128)} %all-to-all-done.1.in_ref), custom_call_target="tpu_custom_call" | custom-call | bytes 16777216 | tf_op jit(solution)/shard_map/pallas_call | solution.py:349
  133.6 1.1 slice.21
  134.9 1.6 broadcast_in_dim.42
  136.4 3.7 %all-to-all-start.3 = ((f32[4,1024,128]{1,2,0:T(8,128)}), f32[4,1024,128]{1,2,0:T(8,128)S(1)}, u32[]{:S(2)}, u32[]{:S(2)}) async-start(f32[4,1024,128]{1,2,0:T(8,128)} %broadcast_in_dim.42), calls=%async_computation.3 | async-start | bytes 4194304 | tf_op jit(solution)/shard_map/all_to_all | solution.py:287
  140.2 1.9 slice.22
  142.1 22.8 %all-to-all-done.3 = f32[4,1024,128]{1,2,0:T(8,128)S(1)} async-done(((f32[4,1024,128]{1,2,0:T(8,128)}), f32[4,1024,128]{1,2,0:T(8,128)S(1)}, u32[]{:S(2)}, u32[]{:S(2)}) %all-to-all-start.3) | async-done | bytes 2097184 | tf_op jit(solution)/shard_map/all_to_all | solution.py:287
  164.9 4.0 %all-to-all-start.4 = ((f32[32,12,8,128]{3,2,1,0:T(8,128)}), f32[32,12,8,128]{3,2,1,0:T(8,128)}, u32[]{:S(2)}, u32[]{:S(2)}) async-start(f32[32,12,8,128]{3,2,1,0:T(8,128)} %shard_map.88), calls=%async_computation.4 | async-start | bytes 3145728 | tf_op jit(solution)/shard_map/all_to_all | solution.py:347
  169.7 52.4 %all-to-all-done.4.in_ref = f32[32,12,8,128]{3,2,1,0:T(8,128)} async-done(((f32[32,12,8,128]{3,2,1,0:T(8,128)}), f32[32,12,8,128]{3,2,1,0:T(8,128)}, u32[]{:S(2)}, u32[]{:S(2)}) %all-to-all-start.4) | async-done | bytes 1572896 | tf_op jit(solution)/shard_map/all_to_all | solution.py:347
  222.1 1.1 broadcast_in_dim.41
  223.2 3.3 %all-to-all-start.2 = ((f32[32,64,128]{2,1,0:T(8,128)}), f32[32,64,128]{2,1,0:T(8,128)S(1)}, u32[]{:S(2)}, u32[]{:S(2)}) async-start(f32[32,64,128]{2,1,0:T(8,128)} %broadcast_in_dim.41), calls=%async_computation.2 | async-start | bytes 2097152 | tf_op jit(solution)/shard_map/all_to_all | solution.py:287
  226.5 8.4 %shard_map.92 = f32[128,1024]{1,0:T(8,128)} custom-call(s32[32,6]{1,0:T(8,128)} %add_select_fusion.runs_ref, s32[1]{0:T(128)} %bitcast.own_ref, f32[32,12,8,128]{3,2,1,0:T(8,128)} %all-to-all-done.4.in_ref), custom_call_target="tpu_custom_call" | custom-call | bytes 1048576 | tf_op jit(solution)/shard_map/pallas_call | solution.py:379
  235.8 17.2 %all-to-all-done.2.pieces_ref = f32[32,64,128]{2,1,0:T(8,128)S(1)} async-done(((f32[32,64,128]{2,1,0:T(8,128)}), f32[32,64,128]{2,1,0:T(8,128)S(1)}, u32[]{:S(2)}, u32[]{:S(2)}) %all-to-all-start.2) | async-done | bytes 1048608 | tf_op jit(solution)/shard_map/all_to_all | solution.py:287
  253.8 3.7 %all-to-all-start.5 = ((f32[8,64,128]{2,1,0:T(8,128)}), f32[8,64,128]{2,1,0:T(8,128)S(1)}, u32[]{:S(2)}, u32[]{:S(2)}) async-start(f32[8,64,128]{2,1,0:T(8,128)} %broadcast_in_dim.43), calls=%async_computation.5 | async-start | bytes 524288 | tf_op jit(solution)/shard_map/all_to_all | solution.py:287
  257.5 33.5 %shard_map.91 = f32[512,512]{1,0:T(8,128)} custom-call(f32[32,64,128]{2,1,0:T(8,128)} %copy-done.6), custom_call_target="tpu_custom_call" | custom-call | flops 536870912 | bytes 20971520 | tf_op jit(solution)/shard_map/pallas_call | solution.py:367
  290.9 5.5 %fusion.15 = f32[512,1024]{1,0:T(8,128)S(1)} fusion(f32[512,512]{1,0:T(8,128)} %shard_map.91, f32[1024,512]{0,1:T(8,128)} %bitcast.31), kind=kOutput, calls=%fused_computation.26 | convolution fusion | flops 3221225472 | bytes 5242880 | tf_op jit(solution)/shard_map/dot_general | solution.py:376
  296.5 1.3 copy-done.2
  297.8 1.5 convolution_subtract_fusion.1
  299.3 13.2 %convolution_subtract_fusion = f32[1024,2048]{1,0:T(8,128)} fusion(f32[1024,2048]{1,0:T(8,128)} %shard_map.90, f32[512,1024]{1,0:T(8,128)} %copy-done.2, f32[512,2048]{1,0:T(8,128)} %all-gather.2.cloned.1.call-done), kind=kOutput, calls=%fused_computation.6 | convolution fusion | flops 6444548096 | bytes 23068672 | tf_op jit(solution)/shard_map/dot_general | solution.py:25
  (34 shorter events, 3.3 us)
Async XLA Ops:
  7.2 10.5 %copy-start = (f32[1,1024,768]{2,1,0:T(8,128)S(1)}, f32[1,1024,768]{2,1,0:T(8,128)}, u32[]{:S(2)}) copy-start(f32[1,1024,768]{2,1,0:T(8,128)} %param.8) | copy-start | bytes 9437188
  12.4 40.1 %all-to-all-start = ((f32[4,6,32,512]{3,2,1,0:T(8,128)}), f32[4,6,32,512]{3,2,1,0:T(8,128)}, u32[]{:S(2)}, u32[]{:S(2)}) async-start(f32[4,6,32,512]{3,2,1,0:T(8,128)} %shard_map.86), calls=%async_computation | async-start | bytes 3145728 | tf_op jit(solution)/shard_map/all_to_all | solution.py:317
  17.6 9.2 %copy-start.11 = (f32[1,1024,1024]{2,1,0:T(8,128)S(1)}, f32[1,1024,1024]{2,1,0:T(8,128)}, u32[]{:S(2)}) copy-start(f32[1,1024,1024]{2,1,0:T(8,128)} %param.7) | copy-start | bytes 12582916
  25.2 1.6 copy-start.3
  26.8 6.9 %copy-start.10 = (f32[1,768]{1,0:T(1,128)S(1)}, f32[1,768]{1,0:T(1,128)}, u32[]{:S(2)}) copy-start(f32[1,768]{1,0:T(1,128)} %param.11) | copy-start | bytes 9220
  26.8 6.9 %copy-start.9 = (f32[1,1024]{1,0:T(1,128)S(1)}, f32[1,1024]{1,0:T(1,128)}, u32[]{:S(2)}) copy-start(f32[1,1024]{1,0:T(1,128)} %param.10) | copy-start | bytes 12292
  33.8 7.0 %copy-start.4 = (f32[1024,768]{1,0:T(8,128)S(1)}, f32[1024,768]{1,0:T(8,128)}, u32[]{:S(2)}) copy-start(f32[1024,768]{1,0:T(8,128)} %copy-done.3) | copy-start | bytes 9437188
  33.8 7.0 %copy-start.8 = (f32[1,768,768]{2,1,0:T(8,128)S(1)}, f32[1,768,768]{2,1,0:T(8,128)}, u32[]{:S(2)}) copy-start(f32[1,768,768]{2,1,0:T(8,128)} %param.9) | copy-start | bytes 7077892
  52.5 61.3 %all-to-all-start.1 = ((f32[32,18,8,128]{3,2,1,0:T(8,128)}), f32[32,18,8,128]{3,2,1,0:T(8,128)}, u32[]{:S(2)}, u32[]{:S(2)}) async-start(f32[32,18,8,128]{3,2,1,0:T(8,128)} %shard_map.89), calls=%async_computation.1 | async-start | bytes 4718592 | tf_op jit(solution)/shard_map/all_to_all | solution.py:331
  136.4 28.4 %all-to-all-start.3 = ((f32[4,1024,128]{1,2,0:T(8,128)}), f32[4,1024,128]{1,2,0:T(8,128)S(1)}, u32[]{:S(2)}, u32[]{:S(2)}) async-start(f32[4,1024,128]{1,2,0:T(8,128)} %broadcast_in_dim.42), calls=%async_computation.3 | async-start | bytes 4194304 | tf_op jit(solution)/shard_map/all_to_all | solution.py:287
  140.2 159.1 %all-gather.2.cloned.1.call-start = ((), (), s32[]{:S(2)}) async-start(), calls=%async_computation.6 | async-start | bytes 4718592 | tf_op jit(solution)/shard_map/all_gather | solution.py:365
  164.9 58.3 %copy-start.5 = (f32[4,1024,128]{1,2,0:T(8,128)}, f32[4,1024,128]{1,2,0:T(8,128)S(1)}, u32[]{:S(2)}) copy-start(f32[4,1024,128]{1,2,0:T(8,128)S(1)} %all-to-all-done.3) | copy-start | bytes 6291460
  164.9 57.2 %all-to-all-start.4 = ((f32[32,12,8,128]{3,2,1,0:T(8,128)}), f32[32,12,8,128]{3,2,1,0:T(8,128)}, u32[]{:S(2)}, u32[]{:S(2)}) async-start(f32[32,12,8,128]{3,2,1,0:T(8,128)} %shard_map.88), calls=%async_computation.4 | async-start | bytes 3145728 | tf_op jit(solution)/shard_map/all_to_all | solution.py:347
  223.2 29.8 %all-to-all-start.2 = ((f32[32,64,128]{2,1,0:T(8,128)}), f32[32,64,128]{2,1,0:T(8,128)S(1)}, u32[]{:S(2)}, u32[]{:S(2)}) async-start(f32[32,64,128]{2,1,0:T(8,128)} %broadcast_in_dim.41), calls=%async_computation.2 | async-start | bytes 2097152 | tf_op jit(solution)/shard_map/all_to_all | solution.py:287
  253.0 4.5 %copy-start.6 = (f32[32,64,128]{2,1,0:T(8,128)}, f32[32,64,128]{2,1,0:T(8,128)S(1)}, u32[]{:S(2)}) copy-start(f32[32,64,128]{2,1,0:T(8,128)S(1)} %all-to-all-done.2.pieces_ref) | copy-start | bytes 3145732
  253.8 42.7 %all-to-all-start.5 = ((f32[8,64,128]{2,1,0:T(8,128)}), f32[8,64,128]{2,1,0:T(8,128)S(1)}, u32[]{:S(2)}, u32[]{:S(2)}) async-start(f32[8,64,128]{2,1,0:T(8,128)} %broadcast_in_dim.43), calls=%async_computation.5 | async-start | bytes 524288 | tf_op jit(solution)/shard_map/all_to_all | solution.py:287
  290.9 6.9 %copy-start.7 = (f32[128,1024]{1,0:T(8,128)S(1)}, f32[128,1024]{1,0:T(8,128)}, u32[]{:S(2)}) copy-start(f32[128,1024]{1,0:T(8,128)} %shard_map.92) | copy-start | bytes 1572868
  296.4 1.3 copy-start.2
  299.3 13.2 %copy-start.1 = (f32[1,1024,768]{2,1,0:T(8,128)S(1)}, f32[1,1024,768]{2,1,0:T(8,128)}, u32[]{:S(2)}) copy-start(f32[1,1024,768]{2,1,0:T(8,128)} %param.8) | copy-start | bytes 9437188
Sparse Core Ops, SparseCore 0:
  142.6 69.3 all-gather.1

commit v2 on v1

v2 whole, which is shorter than its diff:
```python
import functools
import jax
import jax.numpy as jnp
from jax import lax
from jax.experimental import pallas as pl
from jax.experimental.pallas import tpu as pltpu
from jax.sharding import PartitionSpec as P

IDB = 128
SUB = 32
NG = 8192
PANEL = 512
PER_RUN = IDB // SUB
LANES = 128
SUBLANES = 8
GROUPS = SUB // SUBLANES

highest = lax.Precision.HIGHEST
high = lax.Precision.HIGH
shift_value = 0.05
VMEM_LIMIT = 60 * 1024 * 1024


def tdot(left, right, precision):
    return lax.dot_general(left, right, (((0,), (0,)), ((), ())), precision=precision)


class Grid:
    def __init__(self, row_count, col_count):
        self.rows = row_count
        self.cols = col_count
        self.devices = row_count * col_count
        self.row_classes = row_count // PER_RUN
        self.col_classes = col_count // PER_RUN
        self.row_cap = 3
        self.col_cap = 3 + (self.row_classes // self.col_classes - 1) * (3 // (self.row_classes - 1))
        self.slots = self.row_cap * self.col_cap
        evens = list(range(0, row_count, 2))
        halves = [evens[: len(evens) // 2], evens[len(evens) // 2 :]]
        self.order = [e + core for half in halves for core in range(2) for e in half]


def call(kernel, out_shape, in_specs, scratch=(), flops=0, nbytes=0):
    return pl.pallas_call(
        kernel,
        out_shape=out_shape,
        in_specs=in_specs,
        out_specs=jax.tree.map(lambda _: pl.BlockSpec(memory_space=pltpu.VMEM), out_shape),
        scratch_shapes=list(scratch),
        compiler_params=pltpu.CompilerParams(vmem_limit_bytes=VMEM_LIMIT),
        cost_estimate=pl.CostEstimate(flops=flops, bytes_accessed=nbytes, transcendentals=0),
    )


SMEM = pl.BlockSpec(memory_space=pltpu.SMEM)
VMEM = pl.BlockSpec(memory_space=pltpu.VMEM)


def ranks_of(groups, classes):
    kinds = [g % classes for g in groups]
    ranks = []
    for j in range(len(kinds)):
        rank = jnp.int32(0)
        for i in range(j):
            rank = rank + jnp.where(kinds[i] == kinds[j], 1, 0).astype(jnp.int32)
        ranks.append(rank)
    return kinds, ranks


def lane_group():
    return lax.broadcasted_iota(jnp.int32, (SUBLANES, LANES), 1) // SUB


def regroup(ref, row, lanes, turn):
    parts = []
    for g in range(GROUPS):
        start = row + (g - turn + GROUPS) % GROUPS * SUBLANES
        parts.append(ref[pl.ds(pl.multiple_of(start, SUBLANES), SUBLANES), lanes])
    where = lane_group()
    out = []
    for k in range(PER_RUN):
        value = None
        for g in range(GROUPS):
            shift = (g - k) % PER_RUN * SUB
            piece = parts[g] if shift == 0 else pltpu.roll(parts[g], shift, 1)
            value = piece if value is None else jnp.where(where == g, piece, value)
        out.append(value)
    return out


def pack_matrix(grid, runs_ref, own_ref, a_ref, out_ref):
    number = a_ref.shape[0] // IDB
    groups = [runs_ref[own_ref[0], j] for j in range(number)]
    row_kind, row_rank = ranks_of(groups, grid.row_classes)
    col_kind, col_rank = ranks_of(groups, grid.col_classes)
    turn = [g // grid.col_classes % PER_RUN for g in groups]
    if grid.devices * grid.slots != (number * PER_RUN) ** 2:
        out_ref[...] = jnp.zeros_like(out_ref)
    for i in range(number):
        for k in range(PER_RUN):
            for j in range(number):
                lanes = slice(j * IDB, (j + 1) * IDB)
                row = (row_kind[i] * PER_RUN + k) * grid.cols
                slot = row_rank[i] * grid.col_cap + col_rank[j]
                for kk, value in enumerate(regroup(a_ref, i * IDB + k * SUB, lanes, turn[j])):
                    out_ref[row + col_kind[j] * PER_RUN + kk, slot] = value


def pack_modes(grid, per_device, runs_ref, own_ref, y_ref, out_ref):
    number = y_ref.shape[1] // IDB
    groups = [runs_ref[own_ref[0], j] for j in range(number)]
    row_kind, row_rank = ranks_of(groups, grid.row_classes)
    turn = [g // grid.row_classes % PER_RUN for g in groups]
    if grid.devices * grid.row_cap != number * PER_RUN * grid.cols:
        out_ref[...] = jnp.zeros_like(out_ref)
    for m in range(y_ref.shape[0] // SUB):
        for j in range(number):
            lanes = slice(j * IDB, (j + 1) * IDB)
            slot = row_rank[j] * per_device + m % per_device
            for k, value in enumerate(regroup(y_ref, m * SUB, lanes, turn[j])):
                row = (row_kind[j] * PER_RUN + k) * grid.cols + m // per_device
                out_ref[row, slot] = value


def list_places(runs, classes, kind, cap):
    mine = (runs % classes == kind).astype(jnp.int32)
    number = runs.shape[1]
    earlier = jnp.arange(number)[:, None] < jnp.arange(number)[None, :]
    rank = jnp.sum(jnp.where(earlier[None], mine[:, :, None], 0), axis=1)
    hit = (mine[:, :, None] == 1) & (rank[:, :, None] == jnp.arange(cap)[None, None, :])
    return jnp.sum(jnp.where(hit, runs[:, :, None] // classes + 1, 0), axis=1) - 1


def add_blocks(acc_ref, blocks):
    where = lane_group()
    todo = []
    for row, place, value in blocks:
        valid = place >= 0
        place = jnp.maximum(place, 0)
        start = pl.multiple_of(place // PER_RUN * LANES, LANES)
        mask = (where == place % PER_RUN) & valid
        for q in range(GROUPS):
            moved = value if q == 0 else pltpu.roll(value, LANES - q * SUB, 1)
            at = (pl.ds(row + q * SUBLANES, SUBLANES), pl.ds(start, LANES))
            todo.append((at, acc_ref[at] + moved, mask))
    for at, value, mask in todo:
        pltpu.store(acc_ref.at[at], value, mask=mask)


def place_matrix(grid, row_tab, col_tab, in_ref, acc_ref):
    acc_ref[...] = jnp.zeros_like(acc_ref)

    @pl.loop(0, row_tab.shape[0])
    def _(s):
        blocks = []
        for t in range(grid.row_cap):
            row_place = row_tab[s, t]
            row = pl.multiple_of(jnp.maximum(row_place, 0) * SUB, SUB)
            for u in range(grid.col_cap):
                place = jnp.where(row_place >= 0, col_tab[s, u], -1)
                blocks.append((row, place, in_ref[s, t * grid.col_cap + u]))
        add_blocks(acc_ref, blocks)


def place_panel(grid, row_tab, col_tab, in_ref, rows_ref, cols_ref, corner_ref):
    row_limit = rows_ref.shape[0] // SUB
    col_limit = cols_ref.shape[1] // SUB
    rows_ref[...] = jnp.zeros_like(rows_ref)
    cols_ref[...] = jnp.zeros_like(cols_ref)

    @pl.loop(0, row_tab.shape[0])
    def _(s):
        def row_of(t):
            return pl.multiple_of(jnp.maximum(row_tab[s, t], 0) * SUB, SUB)

        for t in range(grid.row_cap):

            @pl.when((row_tab[s, t] >= 0) & (row_tab[s, t] < row_limit))
            def _():
                add_blocks(
                    rows_ref,
                    [(row_of(t), col_tab[s, u], in_ref[s, t * grid.col_cap + u]) for u in range(grid.col_cap)],
                )

        for u in range(grid.col_cap):

            @pl.when((col_tab[s, u] >= 0) & (col_tab[s, u] < col_limit))
            def _():
                add_blocks(
                    cols_ref,
                    [
                        (row_of(t), jnp.where(row_tab[s, t] >= 0, col_tab[s, u], -1), in_ref[s, t * grid.col_cap + u])
                        for t in range(grid.row_cap)
                    ],
                )

    corner_ref[...] = cols_ref[: row_limit * SUB, : col_limit * SUB]


def place_modes(grid, per_device, row_tab, in_ref, acc_ref):
    acc_ref[...] = jnp.zeros_like(acc_ref)

    @pl.loop(0, row_tab.shape[0])
    def _(s):
        blocks = []
        for t in range(grid.row_cap):
            place = row_tab[s, t]
            blocks += [(m * SUB, place, in_ref[s, t * per_device + m]) for m in range(per_device)]
        add_blocks(acc_ref, blocks)


def pick_modes(grid, runs_ref, own_ref, modes_ref, out_ref):
    number = runs_ref.shape[1]
    own_row = own_ref[0] // grid.cols
    own_col = own_ref[0] % grid.cols
    col_kind = own_col // PER_RUN
    if grid.cols * grid.col_cap != number * PER_RUN:
        out_ref[...] = jnp.zeros_like(out_ref)
    for c in range(grid.cols):
        groups = [runs_ref[own_row * grid.cols + (own_col ^ c), j] for j in range(number)]
        kinds, ranks = ranks_of(groups, grid.col_classes)
        for j in range(number):

            @pl.when(kinds[j] == col_kind)
            def _():
                row = pl.multiple_of(groups[j] // grid.col_classes * SUB, SUB)
                out_ref[c, ranks[j]] = modes_ref[pl.ds(row, SUB), :]


def order_modes(grid, runs_ref, own_ref, in_ref, out_ref):
    own_col = own_ref[0] % grid.cols
    number = runs_ref.shape[1]
    groups = [runs_ref[own_ref[0], j] for j in range(number)]
    kinds, ranks = ranks_of(groups, grid.col_classes)
    for j in range(number):
        for k in range(PER_RUN):
            start = j * IDB + k * SUB
            out_ref[start : start + SUB, :] = in_ref[(kinds[j] * PER_RUN + k) ^ own_col, ranks[j]]


def invert_block(matrix):
    n = matrix.shape[0]
    count = n // SUBLANES
    sub = lax.broadcasted_iota(jnp.int32, (SUBLANES, n), 0)
    lane = lax.broadcasted_iota(jnp.int32, (SUBLANES, n), 1)

    def across(value, m):
        return jnp.broadcast_to(value[:, m : m + 1], (SUBLANES, n))

    def down(value, k):
        return jnp.broadcast_to(value[k : k + 1, :], (SUBLANES, n))

    def panel(_, rows):
        head = rows[0]
        split = [across(head, m) for m in range(SUBLANES)]
        for k in range(SUBLANES):
            inverse = 1.0 / down(split[k], k)
            mine = sub == k
            head = jnp.where(lane == k, jnp.where(mine, 1.0, 0.0), head)
            pivot = down(head, k) * inverse
            factor = split[k]
            head = jnp.where(mine, pivot, head - factor * pivot)
            for m in range(k + 1, SUBLANES):
                scaled = down(split[m], k) * inverse
                split[m] = jnp.where(mine, scaled, split[m] - factor * scaled)
        lines = [down(head, m) for m in range(SUBLANES)]
        done = []
        for row in rows[1:]:
            value = jnp.where(lane < SUBLANES, 0.0, row)
            for m in range(SUBLANES):
                value = value - across(row, m) * lines[m]
            done.append(value)
        done.append(head)
        return tuple(pltpu.roll(value, n - SUBLANES, 1) for value in done)

    rows = tuple(matrix[SUBLANES * i : SUBLANES * (i + 1)] for i in range(count))
    rows = lax.fori_loop(0, count, panel, rows)
    return jnp.concatenate(rows, axis=0)


def invert_corner(grid, own_ref, pieces_ref, out_ref, work_ref):
    row_blocks = PANEL // SUB // grid.rows
    col_blocks = PANEL // SUB // grid.cols
    width = col_blocks * SUB
    own_row = own_ref[0] // grid.cols
    own_col = own_ref[0] % grid.cols

    def position(r, b):
        block = r + grid.rows * b
        return pl.multiple_of((((block % grid.cols) ^ own_col) * col_blocks + block // grid.cols) * SUB, SUB)

    for e in range(grid.rows):
        for b in range(row_blocks):
            start = position(own_row ^ e, b)
            for d in range(grid.cols):
                work_ref[pl.ds(start, SUB), d * width : (d + 1) * width] = pieces_ref[
                    d, e, b * SUB : (b + 1) * SUB, :
                ]
    steps = PANEL // LANES
    lane = lax.broadcasted_iota(jnp.int32, (LANES, PANEL), 1) // LANES

    @pl.loop(0, steps)
    def _(step):
        at = pl.ds(pl.multiple_of(step * LANES, LANES), LANES)
        small = invert_block(work_ref[at, at])
        line = jnp.dot(small, work_ref[at, :], precision=highest, preferred_element_type=jnp.float32)
        line = jnp.where(lane == step, jnp.concatenate([small] * steps, axis=1), line)
        for i in range(steps):
            rows = slice(i * LANES, (i + 1) * LANES)
            factor = work_ref[rows, at]
            kept = jnp.where(lane == step, 0.0, work_ref[rows, :])
            update = kept - jnp.dot(
                factor, line, precision=highest, preferred_element_type=jnp.float32
            )
            work_ref[rows, :] = jnp.where(i == step, line, update)

    for i, e in enumerate(grid.order):
        for b in range(row_blocks):
            target = (i * row_blocks + b) * SUB
            out_ref[target : target + SUB, :] = work_ref[pl.ds(position(own_row ^ e, b), SUB), :]


def split(value):
    upper = value.astype(jnp.bfloat16)
    return upper, (value - upper.astype(jnp.float32)).astype(jnp.bfloat16)


def product(left, right):
    total = None
    for i, j in ((0, 1), (1, 0), (0, 0)):
        term = jnp.dot(left[i], right[j], preferred_element_type=jnp.float32)
        total = term if total is None else total + term
    return total


def eliminate_kernel(matrix_ref, solved_ref, *refs):
    parts, out_ref, upper_ref, lower_ref = refs[:-3], refs[-3], refs[-2], refs[-1]

    @pl.when(pl.program_id(0) == 0)
    def _():
        start = 0
        for part in parts:
            rows = slice(start, start + part.shape[0])
            upper_ref[rows, :], lower_ref[rows, :] = split(part[...])
            start += part.shape[0]

    left = split(solved_ref[...])
    width = 256
    for start in range(0, out_ref.shape[1], width):
        at = slice(start, start + width)
        out_ref[:, at] = matrix_ref[:, at] - product(left, (upper_ref[:, at], lower_ref[:, at]))


def eliminate(matrix, solved, parts):
    rows, cols = matrix.shape
    depth = solved.shape[1]
    tile = 256
    return pl.pallas_call(
        eliminate_kernel,
        out_shape=jax.ShapeDtypeStruct((rows, cols), jnp.float32),
        grid=(rows // tile,),
        in_specs=[
            pl.BlockSpec((tile, cols), lambda i: (i, 0)),
            pl.BlockSpec((tile, depth), lambda i: (i, 0)),
        ]
        + [pl.BlockSpec(part.shape, lambda i: (0, 0), pipeline_mode=pl.Buffered(1)) for part in parts],
        out_specs=pl.BlockSpec((tile, cols), lambda i: (i, 0)),
        scratch_shapes=[pltpu.VMEM((depth, cols), jnp.bfloat16)] * 2,
        compiler_params=pltpu.CompilerParams(
            vmem_limit_bytes=VMEM_LIMIT, dimension_semantics=("arbitrary",)
        ),
        cost_estimate=pl.CostEstimate(
            flops=6 * rows * cols * depth, bytes_accessed=12 * rows * cols, transcendentals=0
        ),
    )(matrix, solved, *parts)


def pairs(count, offset):
    return [(i, i ^ offset) for i in range(count)]


def exchange(values, axis, count):
    return [v if d == 0 else lax.ppermute(v, axis, pairs(count, d)) for d, v in enumerate(values)]


def partners(value, axis, count, offsets):
    return [value if d == 0 else lax.ppermute(value, axis, pairs(count, d)) for d in offsets]


def all_rows(value, count):
    both = jnp.stack(partners(value, "row", count, (0, 1)))
    return jnp.concatenate(partners(both, "row", count, range(0, count, 2)))


def line_rows(value, count):
    mine = partners(value, "row", count, range(0, count, 2))
    half = len(mine) // 2
    return jnp.stack(mine[:half]), jnp.stack(mine[half:])


def body(
    inverse_factor,
    coupling,
    boundary_stiffness,
    interior_mass,
    boundary_mass,
    interface_ids,
    trial_modes,
):
    grid = Grid(lax.axis_size("row"), lax.axis_size("col"))
    f32 = jnp.float32
    modes = trial_modes.shape[1]
    mode_count = modes // grid.cols
    per_device = mode_count // SUB
    size = coupling.shape[2]
    local_rows = NG // grid.rows
    local_cols = NG // grid.cols
    runs = interface_ids[:, ::IDB] // IDB
    own = (lax.axis_index("row") * grid.cols + lax.axis_index("col")).astype(jnp.int32).reshape(1)

    factor = inverse_factor[0]
    weighted = jnp.dot(factor, coupling[0], precision=high)
    static = tdot(factor, weighted, high)
    condensed_m = jnp.diag(boundary_mass[0]) + tdot(static, interior_mass[0][:, None] * static, high)
    shifted_s = boundary_stiffness[0] - tdot(weighted, weighted, high) - shift_value * condensed_m

    outbox = call(
        functools.partial(pack_matrix, grid),
        jax.ShapeDtypeStruct((grid.devices, grid.slots, SUBLANES, LANES), f32),
        [SMEM, SMEM, VMEM],
        nbytes=size * size * 8,
    )(runs, own, shifted_s)
    inbox = lax.all_to_all(outbox, ("row", "col"), 0, 0, tiled=True)

    outbox, local_modes, late_runs = lax.optimization_barrier((outbox, trial_modes, runs))
    row_kind = lax.axis_index("row") // PER_RUN
    col_kind = lax.axis_index("col") // PER_RUN
    row_tab = list_places(late_runs, grid.row_classes, row_kind, grid.row_cap)
    col_tab = list_places(late_runs, grid.col_classes, col_kind, grid.col_cap)
    wanted = call(
        functools.partial(pick_modes, grid),
        jax.ShapeDtypeStruct((grid.cols, grid.col_cap, SUB, modes), f32),
        [SMEM, SMEM, VMEM],
        nbytes=trial_modes.size * 8,
    )(runs, own, local_modes)
    wanted = jnp.stack(exchange([wanted[d] for d in range(grid.cols)], "col", grid.cols))
    own_modes = call(
        functools.partial(order_modes, grid),
        jax.ShapeDtypeStruct((size, modes), f32),
        [SMEM, SMEM, VMEM],
        nbytes=size * modes * 8,
    )(runs, own, wanted)
    weighted_modes = tdot(own_modes, condensed_m, high)
    mode_outbox = call(
        functools.partial(pack_modes, grid, per_device),
        jax.ShapeDtypeStruct((grid.devices, grid.row_cap * per_device, SUBLANES, LANES), f32),
        [SMEM, SMEM, VMEM],
        nbytes=size * modes * 8,
    )(runs, own, weighted_modes)

    inbox, mode_outbox = lax.optimization_barrier((inbox, mode_outbox))
    panel_row_count = PANEL // grid.rows
    panel_col_count = PANEL // grid.cols
    row_part, col_part, corner = call(
        functools.partial(place_panel, grid),
        (
            jax.ShapeDtypeStruct((panel_row_count, local_cols), f32),
            jax.ShapeDtypeStruct((local_rows, panel_col_count), f32),
            jax.ShapeDtypeStruct((panel_row_count, panel_col_count), f32),
        ),
        [SMEM, SMEM, VMEM],
        nbytes=size * size * 4,
    )(row_tab, col_tab, inbox)

    pieces = all_rows(corner, grid.rows)
    pieces, row_part, col_part, mode_outbox, inbox = lax.optimization_barrier(
        (pieces, row_part, col_part, mode_outbox, inbox)
    )
    pieces = jnp.stack(partners(pieces, "col", grid.cols, range(grid.cols)))
    line = line_rows(row_part, grid.rows)
    shifted = call(
        functools.partial(place_matrix, grid),
        jax.ShapeDtypeStruct((local_rows, local_cols), f32),
        [SMEM, SMEM, VMEM],
        nbytes=local_rows * local_cols * 8,
    )(row_tab, col_tab, inbox)
    pieces, col_part, mode_outbox, shifted = lax.optimization_barrier(
        (pieces, col_part, mode_outbox, shifted)
    )
    panel_cols = jnp.concatenate(partners(col_part, "col", grid.cols, range(grid.cols)), axis=1)
    mode_inbox = lax.all_to_all(mode_outbox, ("row", "col"), 0, 0, tiled=True)
    inverse = call(
        functools.partial(invert_corner, grid),
        jax.ShapeDtypeStruct((PANEL, PANEL), f32),
        [SMEM, VMEM],
        [pltpu.VMEM((PANEL, PANEL), f32)],
        flops=4 * PANEL**3,
        nbytes=PANEL * PANEL * 80,
    )(own, pieces)
    solved = lax.dot_general(panel_cols, inverse, (((1,), (1,)), ((), ())), precision=highest)
    solved, line = lax.optimization_barrier((solved, line))
    panel_rows = []
    for part in line:
        for stack in partners(part, "row", grid.rows, (0, 1)):
            panel_rows.append(stack.reshape(-1, local_cols))
    solved, mode_inbox = lax.optimization_barrier((solved, mode_inbox))
    modes_local = call(
        functools.partial(place_modes, grid, per_device),
        jax.ShapeDtypeStruct((mode_count, local_rows), f32),
        [SMEM, VMEM],
        nbytes=mode_count * local_rows * 8,
    )(row_tab, mode_inbox)
    panel_modes = modes_local[:, :panel_row_count].T
    panel_modes = jnp.stack(partners(panel_modes, "row", grid.rows, (0, 1)))
    panel_modes, shifted = lax.optimization_barrier((panel_modes, shifted))
    panel_modes = partners(panel_modes, "row", grid.rows, range(0, grid.rows, 2))
    reduced_matrix = eliminate(shifted, solved, panel_rows)
    panel_modes = jnp.concatenate(panel_modes)
    panel_modes = jnp.concatenate([panel_modes[e] for e in grid.order])
    reduced_columns = modes_local - lax.dot_general(
        panel_modes, solved, (((0,), (1,)), ((), ())), precision=high
    )
    return (reduced_matrix, reduced_columns)


def solution(mesh):
    return jax.shard_map(
        body,
        mesh=mesh,
        in_specs=(
            P(("row", "col"), None, None),
            P(("row", "col"), None, None),
            P(("row", "col"), None, None),
            P(("row", "col"), None),
            P(("row", "col"), None),
            P(),
            P("col", None),
        ),
        out_specs=(P("row", "col"), P("col", "row")),
        check_vma=False,
    )
```

time: 320 us -> 305 us (0.953)
  waiting for transfers between devices: 135 us -> 85.8 us
  starting transfers between devices: 26.9 us -> 60.5 us
  between operations: 14.2 us -> 0.87 us
  Pallas kernels: 76.6 us -> 88.4 us
  other arithmetic: 0.63 us -> 11.1 us
  matrix products: 53.3 us -> 43.5 us
    ppermute x0 -> x22, waiting for transfers between devices: none -> 85.8 us  [the longest x19 52.5 us: partners(): lax.ppermute(value, axis, pairs(count, d))]
    all_to_all x1, waiting for transfers between devices: 52.4 us -> 0.01 us  [body(): mode_inbox = lax.all_to_all(mode_outbox, ('row', 'col'), 0, 0, tiled=True)]
    ppermute x0 -> x22, starting transfers between devices: none -> 49 us  [the longest x19 45.5 us: partners(): lax.ppermute(value, axis, pairs(count, d))]
    all_to_all x1, waiting for transfers between devices: 42.9 us -> 0.01 us  [body(): inbox = lax.all_to_all(outbox, ('row', 'col'), 0, 0, tiled=True)]
    all_to_all x4 -> x0, waiting for transfers between devices: 40 us -> none  [the longest x3 40 us: spread(): return lax.all_to_all(copies, axis, 0, 0, tiled=True)]
    pallas_call x0 -> x2, Pallas kernels: none -> 20.4 us  [the longest x1 12.9 us: eliminate(): pl.pallas_call(eliminate_kernel, out_shape=jax.ShapeDtypeStruct((rows, co...]
    all_to_all x4 -> x0, starting transfers between devices: 15.9 us -> none  [the longest x3 10.7 us: spread(): return lax.all_to_all(copies, axis, 0, 0, tiled=True)]
    dot_general x6 -> x4, matrix products: 40.3 us -> 26.2 us  [tdot(): lax.dot_general(left, right, (((0,), (0,)), ((), ())), precision=precision)]
  transfers between devices with their start and end apart: 7 -> 24, of which waited for: 4 -> 11; matrix products, arithmetic and copies ran while one was open for 14% -> 9% of each run, Pallas kernels for 17% -> 25%
where the time goes in v2:
time: 305 us; the launch traced here: 304 us
  Pallas kernels  88.4 us (29%)
  waiting for transfers between devices  85.8 us (28%)
  starting transfers between devices  60.5 us (20%)
  matrix products  43.5 us (14%)
  local copies, waits for them, and re-layouts  14.2 us (5%)
  other arithmetic  11.1 us (4%)
    ppermute x19, waiting for transfers between devices, partners(): lax.ppermute(value, axis, pairs(count, d))  52.5 us
    ppermute x19, starting transfers between devices, partners(): lax.ppermute(value, axis, pairs(count, d))  45.5 us
    pallas_call x1, Pallas kernels, body(): call(functools.partial(invert_corner, grid), jax.ShapeDtypeStruct((PANEL,...  33.5 us
    ppermute x3, waiting for transfers between devices, exchange(): lax.ppermute(v, axis, pairs(count, d))  33.3 us
    dot_general x4, matrix products, tdot(): lax.dot_general(left, right, (((0,), (0,)), ((), ())), precision=precision)  26.2 us
    pallas_call x1, Pallas kernels, body(): call(functools.partial(place_matrix, grid), jax.ShapeDtypeStruct((local_r...  13.7 us
    pallas_call x1, Pallas kernels, eliminate(): pl.pallas_call(eliminate_kernel, out_shape=jax.ShapeDtypeStruct((rows, co...  12.9 us
    dot_general x1, matrix products, body(): weighted = jnp.dot(factor, coupling[0], precision=high)  7.54 us
  transfers between devices with their start and end apart: 24, of which 11 were waited for; matrix products, arithmetic and copies ran while one was open for 9% of the time, Pallas kernels for 25%

profile of v2, /device:TPU:0, one launch (start us, length us, event | category | flops | bytes accessed | tf_op | source)
XLA Modules:
  0.0 304.4 jit_solution(4534869911571276854)
XLA Ops:
  2.6 7.5 %fusion.4 = f32[1024,768]{1,0:T(8,128)S(1)} fusion(f32[1,1024,1024]{2,1,0:T(8,128)} %param.7, f32[1,1024,768]{2,1,0:T(8,128)S(1)} %copy-done), kind=kOutput, calls=%fused_computation.4 | convolution fusion | flops 4831838208 | bytes 10485760 | tf_op jit(solution)/shard_map/dot_general | solution.py:422
  11.8 6.9 %fusion.2 = f32[768,1024]{1,0:T(8,128)} fusion(f32[1024,768]{1,0:T(8,128)S(1)} %fusion.4, f32[1,1024,1024]{2,1,0:T(8,128)S(1)} %copy-done.14), kind=kOutput, calls=%fused_computation.2 | convolution fusion | flops 4831838208 | bytes 10485760 | tf_op jit(solution)/shard_map/dot_general | solution.py:25
  18.7 6.9 %fusion = f32[768,768]{1,0:T(8,128)S(1)} fusion(f32[768,1024]{1,0:T(8,128)} %fusion.2, f32[1024]{0:T(1024)S(1)} %bitcast.77), kind=kOutput, calls=%fused_computation | convolution fusion | flops 3624665088 | bytes 5509120 | tf_op jit(solution)/shard_map/dot_general | solution.py:25
  25.7 6.8 %fusion.7.a_ref = f32[768,768]{1,0:T(8,128)} fusion(f32[1,768,768]{2,1,0:T(8,128)S(1)} %copy-done.8, f32[768,768]{1,0:T(8,128)S(1)} %fusion, f32[1024,768]{1,0:T(8,128)S(1)} %copy-done.5, f32[768]{0:T(1024)S(1)} %reduce.1), kind=kOutput, calls=%fused_computation.8 | convolution fusion | flops 3627417600 | bytes 10226688 | tf_op jit(solution)/shard_map/dot_general | solution.py:25
  32.5 5.0 %shard_map.86 = f32[32,18,8,128]{3,2,1,0:T(8,128)} custom-call(s32[32,6]{1,0:T(8,128)} %add_select_fusion.2.runs_ref, s32[1]{0:T(128)} %bitcast.own_ref, f32[768,768]{1,0:T(8,128)} %fusion.7.a_ref), custom_call_target="tpu_custom_call" | custom-call | bytes 4718592 | tf_op jit(solution)/shard_map/pallas_call | solution.py:427
  37.5 7.3 %all-to-all-start = ((f32[32,18,8,128]{3,2,1,0:T(8,128)}), f32[32,18,8,128]{3,2,1,0:T(8,128)S(1)}, u32[]{:S(2)}, u32[]{:S(2)}) async-start(f32[32,18,8,128]{3,2,1,0:T(8,128)} %shard_map.86), calls=%async_computation | async-start | bytes 4718592 | tf_op jit(solution)/shard_map/all_to_all | solution.py:433
  44.8 3.5 %shard_map.87 = f32[4,6,32,512]{3,2,1,0:T(8,128)} custom-call(s32[32,6]{1,0:T(8,128)} %add_select_fusion.2.runs_ref, s32[1]{0:T(128)} %bitcast.own_ref, f32[2048,512]{1,0:T(8,128)} %modes_ref), custom_call_target="tpu_custom_call" | custom-call | bytes 8388608 | tf_op jit(solution)/shard_map/pallas_call | solution.py:440
  48.3 2.4 fusion.32
  50.8 2.7 collective-permute-start.2
  56.2 25.3 %collective-permute-done.2 = f32[6,32,512]{2,1,0:T(8,128)} collective-permute-done((f32[6,32,512]{2,1,0:T(8,128)}, f32[6,32,512]{2,1,0:T(8,128)}, u32[]{:S(2)}, u32[]{:S(2)}) %collective-permute-start.2) | collective-permute-done | bytes 393248 | tf_op jit(solution)/shard_map/ppermute | solution.py:383
  81.6 5.6 %collective-permute-done.1 = f32[6,32,512]{2,1,0:T(8,128)} collective-permute-done((f32[6,32,512]{2,1,0:T(8,128)}, f32[6,32,512]{2,1,0:T(8,128)}, u32[]{:S(2)}, u32[]{:S(2)}) %collective-permute-start.1) | collective-permute-done | bytes 393248 | tf_op jit(solution)/shard_map/ppermute | solution.py:383
  89.5 2.6 pad_maximum_fusion.in_ref
  92.1 2.7 shard_map.88
  94.8 5.6 %fusion.16.y_ref = f32[512,768]{1,0:T(8,128)} fusion(f32[768,512]{1,0:T(8,128)} %shard_map.88, f32[768,768]{1,0:T(8,128)} %copy-done.3, f32[768]{0:T(1024)S(1)} %reduce.1), kind=kOutput, calls=%fused_computation.19 | convolution fusion | flops 1813708800 | bytes 5508096 | tf_op jit(solution)/shard_map/dot_general | solution.py:25
  100.5 3.9 %shard_map.89 = f32[32,12,8,128]{3,2,1,0:T(8,128)} custom-call(s32[32,6]{1,0:T(8,128)} %add_select_fusion.2.runs_ref, s32[1]{0:T(128)} %bitcast.own_ref, f32[512,768]{1,0:T(8,128)} %fusion.16.y_ref), custom_call_target="tpu_custom_call" | custom-call | bytes 3145728 | tf_op jit(solution)/shard_map/pallas_call | solution.py:454
  105.8 7.5 %shard_map.90 = (f32[64,2048]{1,0:T(8,128)}, f32[1024,128]{1,0:T(8,128)}, f32[64,128]{1,0:T(8,128)}) custom-call(s32[32,3]{1,0:T(8,128)} %broadcast_add_fusion.row_tab, s32[32,6]{1,0:T(8,128)} %broadcast_add_fusion.1.col_tab, f32[32,18,8,128]{3,2,1,0:T(8,128)} %copy-done.2), custom_call_target="tpu_custom_call" | custom-call | bytes 2359296 | tf_op jit(solution)/shard_map/pallas_call | solution.py:464
  115.5 4.0 %collective-permute-start.6 = (f32[2,64,128]{2,1,0:T(8,128)S(1)}, f32[2,64,128]{2,1,0:T(8,128)S(1)}, u32[]{:S(2)}, u32[]{:S(2)}) collective-permute-start(f32[2,64,128]{2,1,0:T(8,128)S(1)} %pad_maximum_fusion.5), channel_id=1, source_target_pairs={{0,24},{4,28},{8,16},{12,20},{16,8},{20,12},{24,0},{28,4},{1,25},{... | collective-permute-start | bytes 196616 | tf_op jit(solution)/shard_map/ppermute | solution.py:387
  120.2 3.8 %collective-permute-done.4 = f32[2,64,128]{2,1,0:T(8,128)S(1)} collective-permute-done((f32[2,64,128]{2,1,0:T(8,128)S(1)}, f32[2,64,128]{2,1,0:T(8,128)S(1)}, u32[]{:S(2)}, u32[]{:S(2)}) %collective-permute-start.4) | collective-permute-done | bytes 65568 | tf_op jit(solution)/shard_map/ppermute | solution.py:387
  126.1 2.6 collective-permute-start.9
  129.7 13.7 %shard_map.91.matrix_ref = f32[1024,2048]{1,0:T(8,128)} custom-call(s32[32,3]{1,0:T(8,128)} %broadcast_add_fusion.row_tab, s32[32,6]{1,0:T(8,128)} %broadcast_add_fusion.1.col_tab, f32[32,18,8,128]{3,2,1,0:T(8,128)} %copy-done.2), custom_call_target="tpu_custom_call" | custom-call | bytes 16777216 | tf_op jit(solution)/shard_map/pallas_call | solution.py:481
  144.5 4.2 %all-to-all-start.1 = ((f32[32,12,8,128]{3,2,1,0:T(8,128)}), f32[32,12,8,128]{3,2,1,0:T(8,128)S(1)}, u32[]{:S(2)}, u32[]{:S(2)}) async-start(f32[32,12,8,128]{3,2,1,0:T(8,128)} %shard_map.89), calls=%async_computation.1 | async-start | bytes 3145728 | tf_op jit(solution)/shard_map/all_to_all | solution.py:491
  148.7 3.4 %collective-permute-start.15 = (f32[64,2048]{1,0:T(8,128)}, f32[64,2048]{1,0:T(8,128)S(1)}, u32[]{:S(2)}, u32[]{:S(2)}) collective-permute-start(f32[64,2048]{1,0:T(8,128)} %get-tuple-element.38), channel_id=1, source_target_pairs={{0,24},{4,28},{8,16},{12,20},{16,8},{20,12},{24,0},{28,4},{1,25},{... | collective-permute-start | bytes 1572872 | tf_op jit(solution)/shard_map/ppermute | solution.py:387
  153.1 2.4 collective-permute-start.12
  156.1 34.2 %collective-permute-done.15 = f32[64,2048]{1,0:T(8,128)S(1)} collective-permute-done((f32[64,2048]{1,0:T(8,128)}, f32[64,2048]{1,0:T(8,128)S(1)}, u32[]{:S(2)}, u32[]{:S(2)}) %collective-permute-start.15) | collective-permute-done | bytes 524320 | tf_op jit(solution)/shard_map/ppermute | solution.py:387
  192.0 33.5 %shard_map.92 = f32[512,512]{1,0:T(8,128)} custom-call(s32[1]{0:T(128)} %bitcast.own_ref, f32[4,8,64,128]{3,2,1,0:T(8,128)} %pad_maximum_fusion.1.pieces_ref), custom_call_target="tpu_custom_call" | custom-call | flops 536870912 | bytes 20971520 | tf_op jit(solution)/shard_map/pallas_call | solution.py:492
  225.5 5.5 %collective-permute-done.14 = f32[64,2048]{1,0:T(8,128)} collective-permute-done((f32[64,2048]{1,0:T(8,128)}, f32[64,2048]{1,0:T(8,128)}, u32[]{:S(2)}, u32[]{:S(2)}) %collective-permute-start.14) | collective-permute-done | bytes 524320 | tf_op jit(solution)/shard_map/ppermute | solution.py:387
  235.6 6.1 %fusion.8.solved_ref = f32[1024,512]{1,0:T(8,128)} fusion(f32[512,512]{1,0:T(8,128)S(1)} %copy-done.7, f32[1024,128]{1,0:T(8,128)S(1)} %collective-permute-done.12, f32[1024,128]{1,0:T(8,128)} %collective-permute-done.11, f32[1024,128]{1,0:T(8,128)} %collective-permute-done.10, f32[1024,128]{1,0:T(8,128)S(1)} %copy-done.10), kind=kOutput, calls=%fused_computation.11 | convolution fusion | flops 3222798336 | bytes 5242880 | tf_op jit(solution)/shard_map/dot_general | solution.py:500
  243.3 5.7 %shard_map.93 = f32[128,1024]{1,0:T(8,128)} custom-call(s32[32,3]{1,0:T(8,128)} %broadcast_add_fusion.row_tab, f32[32,12,8,128]{3,2,1,0:T(8,128)} %copy-done.6), custom_call_target="tpu_custom_call" | custom-call | bytes 1048576 | tf_op jit(solution)/shard_map/pallas_call | solution.py:507
  251.2 24.3 %collective-permute-start.20 = (f32[2,64,128]{1,2,0:T(8,128)S(1)}, f32[2,64,128]{1,2,0:T(8,128)S(1)}, u32[]{:S(2)}, u32[]{:S(2)}) collective-permute-start(f32[2,64,128]{1,2,0:T(8,128)S(1)} %pad_maximum_fusion.4), channel_id=1, source_target_pairs={{0,16},{4,20},{8,24},{12,28},{16,0},{20,4},{24,8},{28,12},{1,17},{... | collective-permute-start | bytes 196616 | tf_op jit(solution)/shard_map/ppermute | solution.py:387
  276.5 12.9 %shard_map.94 = f32[1024,2048]{1,0:T(8,128)} custom-call(f32[1024,2048]{1,0:T(8,128)} %shard_map.91.matrix_ref, f32[1024,512]{1,0:T(8,128)} %fusion.8.solved_ref, f32[128,2048]{1,0:T(8,128)} %bitcast.24.refs_0_, f32[128,2048]{1,0:T(8,128)} %bitcast.78, f32[128,2048]{1,0:T(8,128)} %bitcast.26.refs_2_, f32[128,2048]{1,0:T(8,128)} %bitcast.27.refs_3_), custom_call_target="tpu_custom_call" | custom-call | flops 6442450944 | bytes 25165824 | tf_op jit(solution)/shard_map/pallas_call | solution.py:358
  295.4 3.5 %collective-permute-done.21 = f32[2,64,128]{1,2,0:T(8,128)S(1)} collective-permute-done((f32[2,64,128]{1,2,0:T(8,128)S(1)}, f32[2,64,128]{1,2,0:T(8,128)S(1)}, u32[]{:S(2)}, u32[]{:S(2)}) %collective-permute-start.21) | collective-permute-done | bytes 65568 | tf_op jit(solution)/shard_map/ppermute | solution.py:387
  300.8 3.6 %convolution_subtract_fusion = f32[128,1024]{1,0:T(8,128)} fusion(f32[128,1024]{1,0:T(8,128)} %shard_map.93, f32[512,128]{0,1:T(8,128)S(1)} %concatenate.12, f32[1024,512]{1,0:T(8,128)} %fusion.8.solved_ref), kind=kOutput, calls=%fused_computation.22 | convolution fusion | flops 402784256 | bytes 3407872 | tf_op jit(solution)/shard_map/dot_general | solution.py:520
  (100 shorter events, 37.8 us)
Async XLA Ops:
  2.6 9.2 %copy-start.14 = (f32[1,1024,1024]{2,1,0:T(8,128)S(1)}, f32[1,1024,1024]{2,1,0:T(8,128)}, u32[]{:S(2)}) copy-start(f32[1,1024,1024]{2,1,0:T(8,128)} %param.7) | copy-start | bytes 12582916
  11.8 6.9 %copy-start.13 = (f32[1,768]{1,0:T(1,128)S(1)}, f32[1,768]{1,0:T(1,128)}, u32[]{:S(2)}) copy-start(f32[1,768]{1,0:T(1,128)} %param.11) | copy-start | bytes 9220
  11.8 6.9 %copy-start.12 = (f32[1,1024]{1,0:T(1,128)S(1)}, f32[1,1024]{1,0:T(1,128)}, u32[]{:S(2)}) copy-start(f32[1,1024]{1,0:T(1,128)} %param.10) | copy-start | bytes 12292
  18.7 7.0 %copy-start.5 = (f32[1024,768]{1,0:T(8,128)S(1)}, f32[1024,768]{1,0:T(8,128)}, u32[]{:S(2)}) copy-start(f32[1024,768]{1,0:T(8,128)} %copy-done.4) | copy-start | bytes 9437188
  18.7 7.0 %copy-start.8 = (f32[1,768,768]{2,1,0:T(8,128)S(1)}, f32[1,768,768]{2,1,0:T(8,128)}, u32[]{:S(2)}) copy-start(f32[1,768,768]{2,1,0:T(8,128)} %param.9) | copy-start | bytes 7077892
  37.5 66.9 %all-to-all-start = ((f32[32,18,8,128]{3,2,1,0:T(8,128)}), f32[32,18,8,128]{3,2,1,0:T(8,128)S(1)}, u32[]{:S(2)}, u32[]{:S(2)}) async-start(f32[32,18,8,128]{3,2,1,0:T(8,128)} %shard_map.86), calls=%async_computation | async-start | bytes 4718592 | tf_op jit(solution)/shard_map/all_to_all | solution.py:433
  50.8 30.8 %collective-permute-start.2 = (f32[6,32,512]{2,1,0:T(8,128)}, f32[6,32,512]{2,1,0:T(8,128)}, u32[]{:S(2)}, u32[]{:S(2)}) collective-permute-start(f32[6,32,512]{2,1,0:T(8,128)} %get-tuple-element.51), channel_id=1, source_target_pairs={{0,3},{1,2},{2,1},{3,0},{4,7},{5,6},{6,5},{7,4},{8,11},{9,10},{10,... | collective-permute-start | bytes 1179656 | tf_op jit(solution)/shard_map/ppermute | solution.py:383
  53.4 33.7 %collective-permute-start.1 = (f32[6,32,512]{2,1,0:T(8,128)}, f32[6,32,512]{2,1,0:T(8,128)}, u32[]{:S(2)}, u32[]{:S(2)}) collective-permute-start(f32[6,32,512]{2,1,0:T(8,128)} %get-tuple-element.52), channel_id=1, source_target_pairs={{0,2},{1,3},{2,0},{3,1},{4,6},{5,7},{6,4},{7,5},{8,10},{9,11},{10,... | collective-permute-start | bytes 1179656 | tf_op jit(solution)/shard_map/ppermute | solution.py:383
  54.0 35.5 %collective-permute-start = (f32[6,32,512]{2,1,0:T(8,128)S(1)}, f32[6,32,512]{2,1,0:T(8,128)}, u32[]{:S(2)}, u32[]{:S(2)}) collective-permute-start(f32[6,32,512]{2,1,0:T(8,128)S(1)} %get-tuple-element.53), channel_id=1, source_target_pairs={{0,1},{1,0},{2,3},{3,2},{4,5},{5,4},{6,7},{7,6},{8,9},{9,8},{10,11... | collective-permute-start | bytes 1179656 | tf_op jit(solution)/shard_map/ppermute | solution.py:383
  113.3 1.4 collective-permute-start.3
  115.5 10.6 %collective-permute-start.6 = (f32[2,64,128]{2,1,0:T(8,128)S(1)}, f32[2,64,128]{2,1,0:T(8,128)S(1)}, u32[]{:S(2)}, u32[]{:S(2)}) collective-permute-start(f32[2,64,128]{2,1,0:T(8,128)S(1)} %pad_maximum_fusion.5), channel_id=1, source_target_pairs={{0,24},{4,28},{8,16},{12,20},{16,8},{20,12},{24,0},{28,4},{1,25},{... | collective-permute-start | bytes 196616 | tf_op jit(solution)/shard_map/ppermute | solution.py:387
  119.5 6.6 %collective-permute-start.5 = (f32[2,64,128]{2,1,0:T(8,128)S(1)}, f32[2,64,128]{2,1,0:T(8,128)S(1)}, u32[]{:S(2)}, u32[]{:S(2)}) collective-permute-start(f32[2,64,128]{2,1,0:T(8,128)S(1)} %pad_maximum_fusion.5), channel_id=1, source_target_pairs={{0,16},{4,20},{8,24},{12,28},{16,0},{20,4},{24,8},{28,12},{1,17},{... | collective-permute-start | bytes 196616 | tf_op jit(solution)/shard_map/ppermute | solution.py:387
  119.6 4.3 %collective-permute-start.4 = (f32[2,64,128]{2,1,0:T(8,128)S(1)}, f32[2,64,128]{2,1,0:T(8,128)S(1)}, u32[]{:S(2)}, u32[]{:S(2)}) collective-permute-start(f32[2,64,128]{2,1,0:T(8,128)S(1)} %pad_maximum_fusion.5), channel_id=1, source_target_pairs={{0,8},{4,12},{8,0},{12,4},{16,24},{20,28},{24,16},{28,20},{1,9},{5... | collective-permute-start | bytes 196616 | tf_op jit(solution)/shard_map/ppermute | solution.py:387
  126.1 17.3 %collective-permute-start.9 = (f32[8,64,128]{2,1,0:T(8,128)S(1)}, f32[8,64,128]{2,1,0:T(8,128)S(1)}, u32[]{:S(2)}, u32[]{:S(2)}) collective-permute-start(f32[8,64,128]{2,1,0:T(8,128)S(1)} %constant_dynamic-update-slice_fusion), channel_id=1, source_target_pairs={{0,3},{1,2},{2,1},{3,0},{4,7},{5,6},{6,5},{7,4},{8,11},{9,10},{10,... | collective-permute-start | bytes 786440 | tf_op jit(solution)/shard_map/ppermute | solution.py:387
  128.7 14.7 %collective-permute-start.8 = (f32[8,64,128]{2,1,0:T(8,128)S(1)}, f32[8,64,128]{2,1,0:T(8,128)S(1)}, u32[]{:S(2)}, u32[]{:S(2)}) collective-permute-start(f32[8,64,128]{2,1,0:T(8,128)S(1)} %constant_dynamic-update-slice_fusion), channel_id=1, source_target_pairs={{0,2},{1,3},{2,0},{3,1},{4,6},{5,7},{6,4},{7,5},{8,10},{9,11},{10,... | collective-permute-start | bytes 786440 | tf_op jit(solution)/shard_map/ppermute | solution.py:387
  128.7 14.7 %collective-permute-start.7 = (f32[8,64,128]{2,1,0:T(8,128)S(1)}, f32[8,64,128]{2,1,0:T(8,128)S(1)}, u32[]{:S(2)}, u32[]{:S(2)}) collective-permute-start(f32[8,64,128]{2,1,0:T(8,128)S(1)} %constant_dynamic-update-slice_fusion), channel_id=1, source_target_pairs={{0,1},{1,0},{2,3},{3,2},{4,5},{5,4},{6,7},{7,6},{8,9},{9,8},{10,11... | collective-permute-start | bytes 786440 | tf_op jit(solution)/shard_map/ppermute | solution.py:387
  143.4 9.7 %copy-start.10 = (f32[1024,128]{1,0:T(8,128)S(1)}, f32[1024,128]{1,0:T(8,128)}, u32[]{:S(2)}) copy-start(f32[1024,128]{1,0:T(8,128)} %get-tuple-element.36) | copy-start | bytes 1572868
  144.5 97.7 %all-to-all-start.1 = ((f32[32,12,8,128]{3,2,1,0:T(8,128)}), f32[32,12,8,128]{3,2,1,0:T(8,128)S(1)}, u32[]{:S(2)}, u32[]{:S(2)}) async-start(f32[32,12,8,128]{3,2,1,0:T(8,128)} %shard_map.89), calls=%async_computation.1 | async-start | bytes 3145728 | tf_op jit(solution)/shard_map/all_to_all | solution.py:491
  148.7 41.6 %collective-permute-start.15 = (f32[64,2048]{1,0:T(8,128)}, f32[64,2048]{1,0:T(8,128)S(1)}, u32[]{:S(2)}, u32[]{:S(2)}) collective-permute-start(f32[64,2048]{1,0:T(8,128)} %get-tuple-element.38), channel_id=1, source_target_pairs={{0,24},{4,28},{8,16},{12,20},{16,8},{20,12},{24,0},{28,4},{1,25},{... | collective-permute-start | bytes 1572872 | tf_op jit(solution)/shard_map/ppermute | solution.py:387
  152.1 78.9 %collective-permute-start.14 = (f32[64,2048]{1,0:T(8,128)}, f32[64,2048]{1,0:T(8,128)}, u32[]{:S(2)}, u32[]{:S(2)}) collective-permute-start(f32[64,2048]{1,0:T(8,128)} %get-tuple-element.38), channel_id=1, source_target_pairs={{0,16},{4,20},{8,24},{12,28},{16,0},{20,4},{24,8},{28,12},{1,17},{... | collective-permute-start | bytes 1572872 | tf_op jit(solution)/shard_map/ppermute | solution.py:387
  152.1 81.2 %collective-permute-start.13 = (f32[64,2048]{1,0:T(8,128)}, f32[64,2048]{1,0:T(8,128)}, u32[]{:S(2)}, u32[]{:S(2)}) collective-permute-start(f32[64,2048]{1,0:T(8,128)} %get-tuple-element.38), channel_id=1, source_target_pairs={{0,8},{4,12},{8,0},{12,4},{16,24},{20,28},{24,16},{28,20},{1,9},{5... | collective-permute-start | bytes 1572872 | tf_op jit(solution)/shard_map/ppermute | solution.py:387
  153.1 82.5 %collective-permute-start.12 = (f32[1024,128]{1,0:T(8,128)S(1)}, f32[1024,128]{1,0:T(8,128)S(1)}, u32[]{:S(2)}, u32[]{:S(2)}) collective-permute-start(f32[1024,128]{1,0:T(8,128)S(1)} %copy-done.10), channel_id=1, source_target_pairs={{0,3},{1,2},{2,1},{3,0},{4,7},{5,6},{6,5},{7,4},{8,11},{9,10},{10,... | collective-permute-start | bytes 1572872 | tf_op jit(solution)/shard_map/ppermute | solution.py:387
  155.6 80.1 %collective-permute-start.11 = (f32[1024,128]{1,0:T(8,128)S(1)}, f32[1024,128]{1,0:T(8,128)}, u32[]{:S(2)}, u32[]{:S(2)}) collective-permute-start(f32[1024,128]{1,0:T(8,128)S(1)} %copy-done.10), channel_id=1, source_target_pairs={{0,2},{1,3},{2,0},{3,1},{4,6},{5,7},{6,4},{7,5},{8,10},{9,11},{10,... | collective-permute-start | bytes 1572872 | tf_op jit(solution)/shard_map/ppermute | solution.py:387
  190.3 45.3 %collective-permute-start.10 = (f32[1024,128]{1,0:T(8,128)S(1)}, f32[1024,128]{1,0:T(8,128)}, u32[]{:S(2)}, u32[]{:S(2)}) collective-permute-start(f32[1024,128]{1,0:T(8,128)S(1)} %copy-done.10), channel_id=1, source_target_pairs={{0,1},{1,0},{2,3},{3,2},{4,5},{5,4},{6,7},{7,6},{8,9},{9,8},{10,11... | collective-permute-start | bytes 1572872 | tf_op jit(solution)/shard_map/ppermute | solution.py:387
  225.5 10.1 %copy-start.7 = (f32[512,512]{1,0:T(8,128)S(1)}, f32[512,512]{1,0:T(8,128)}, u32[]{:S(2)}) copy-start(f32[512,512]{1,0:T(8,128)} %shard_map.92) | copy-start | bytes 3145732
  241.7 33.8 %collective-permute-start.17 = (f32[2,64,2048]{2,1,0:T(8,128)}, f32[2,64,2048]{2,1,0:T(8,128)S(1)}, u32[]{:S(2)}, u32[]{:S(2)}) collective-permute-start(f32[2,64,2048]{2,1,0:T(8,128)} %pad_maximum_fusion.2), channel_id=1, source_target_pairs={{0,4},{4,0},{8,12},{12,8},{16,20},{20,16},{24,28},{28,24},{1,5},{5... | collective-permute-start | bytes 3145736 | tf_op jit(solution)/shard_map/ppermute | solution.py:387
  241.7 33.8 %collective-permute-start.18 = (f32[2,64,2048]{2,1,0:T(8,128)}, f32[2,64,2048]{2,1,0:T(8,128)}, u32[]{:S(2)}, u32[]{:S(2)}) collective-permute-start(f32[2,64,2048]{2,1,0:T(8,128)} %pad_maximum_fusion.3), channel_id=1, source_target_pairs={{0,4},{4,0},{8,12},{12,8},{16,20},{20,16},{24,28},{28,24},{1,5},{5... | collective-permute-start | bytes 3145736 | tf_op jit(solution)/shard_map/ppermute | solution.py:387
  249.9 1.3 collective-permute-start.16
  251.2 41.4 %collective-permute-start.20 = (f32[2,64,128]{1,2,0:T(8,128)S(1)}, f32[2,64,128]{1,2,0:T(8,128)S(1)}, u32[]{:S(2)}, u32[]{:S(2)}) collective-permute-start(f32[2,64,128]{1,2,0:T(8,128)S(1)} %pad_maximum_fusion.4), channel_id=1, source_target_pairs={{0,16},{4,20},{8,24},{12,28},{16,0},{20,4},{24,8},{28,12},{1,17},{... | collective-permute-start | bytes 196616 | tf_op jit(solution)/shard_map/ppermute | solution.py:387
  289.4 5.4 %collective-permute-start.19 = (f32[2,64,128]{1,2,0:T(8,128)S(1)}, f32[2,64,128]{1,2,0:T(8,128)S(1)}, u32[]{:S(2)}, u32[]{:S(2)}) collective-permute-start(f32[2,64,128]{1,2,0:T(8,128)S(1)} %pad_maximum_fusion.4), channel_id=1, source_target_pairs={{0,8},{4,12},{8,0},{12,4},{16,24},{20,28},{24,16},{28,20},{1,9},{5... | collective-permute-start | bytes 196616 | tf_op jit(solution)/shard_map/ppermute | solution.py:387
  290.2 8.8 %collective-permute-start.21 = (f32[2,64,128]{1,2,0:T(8,128)S(1)}, f32[2,64,128]{1,2,0:T(8,128)S(1)}, u32[]{:S(2)}, u32[]{:S(2)}) collective-permute-start(f32[2,64,128]{1,2,0:T(8,128)S(1)} %pad_maximum_fusion.4), channel_id=1, source_target_pairs={{0,24},{4,28},{8,16},{12,20},{16,8},{20,12},{24,0},{28,4},{1,25},{... | collective-permute-start | bytes 196616 | tf_op jit(solution)/shard_map/ppermute | solution.py:387
  292.6 11.8 %copy-start.1 = (f32[1,1024,768]{2,1,0:T(8,128)S(1)}, f32[1,1024,768]{2,1,0:T(8,128)}, u32[]{:S(2)}) copy-start(f32[1,1024,768]{2,1,0:T(8,128)} %param.8) | copy-start | bytes 9437188
  (8 other events, 21.6 us)

commit v3 on v2

--- a/solution.py
+++ b/solution.py
@@ -18,7 +18,7 @@
 highest = lax.Precision.HIGHEST
 high = lax.Precision.HIGH
 shift_value = 0.05
-VMEM_LIMIT = 60 * 1024 * 1024
+MIB = 1024 * 1024
 
 
 def tdot(left, right, precision):
@@ -35,19 +35,16 @@
         self.row_cap = 3
         self.col_cap = 3 + (self.row_classes // self.col_classes - 1) * (3 // (self.row_classes - 1))
         self.slots = self.row_cap * self.col_cap
-        evens = list(range(0, row_count, 2))
-        halves = [evens[: len(evens) // 2], evens[len(evens) // 2 :]]
-        self.order = [e + core for half in halves for core in range(2) for e in half]
-
-
-def call(kernel, out_shape, in_specs, scratch=(), flops=0, nbytes=0):
+
+
+def call(kernel, out_shape, in_specs, scratch=(), flops=0, nbytes=0, limit=20):
     return pl.pallas_call(
         kernel,
         out_shape=out_shape,
         in_specs=in_specs,
         out_specs=jax.tree.map(lambda _: pl.BlockSpec(memory_space=pltpu.VMEM), out_shape),
         scratch_shapes=list(scratch),
-        compiler_params=pltpu.CompilerParams(vmem_limit_bytes=VMEM_LIMIT),
+        compiler_params=pltpu.CompilerParams(vmem_limit_bytes=limit * MIB),
         cost_estimate=pl.CostEstimate(flops=flops, bytes_accessed=nbytes, transcendentals=0),
     )
 
@@ -314,9 +311,9 @@
             )
             work_ref[rows, :] = jnp.where(i == step, line, update)
 
-    for i, e in enumerate(grid.order):
+    for e in range(grid.rows):
         for b in range(row_blocks):
-            target = (i * row_blocks + b) * SUB
+            target = (e * row_blocks + b) * SUB
             out_ref[target : target + SUB, :] = work_ref[pl.ds(position(own_row ^ e, b), SUB), :]
 
 
@@ -333,8 +330,8 @@
     return total
 
 
-def eliminate_kernel(matrix_ref, solved_ref, *refs):
-    parts, out_ref, upper_ref, lower_ref = refs[:-3], refs[-3], refs[-2], refs[-1]
+def eliminate_kernel(skip, matrix_ref, solved_ref, *refs):
+    parts, out_ref, upper_ref, lower_ref = refs[skip:-3], refs[-3], refs[-2], refs[-1]
 
     @pl.when(pl.program_id(0) == 0)
     def _():
@@ -351,28 +348,32 @@
         out_ref[:, at] = matrix_ref[:, at] - product(left, (upper_ref[:, at], lower_ref[:, at]))
 
 
-def eliminate(matrix, solved, parts):
+def eliminate(matrix, solved, parts, half, into=()):
     rows, cols = matrix.shape
     depth = solved.shape[1]
-    tile = 256
+    tile = 256 if rows % 512 == 0 else rows // 2
+    tiles = rows // 2 // tile
+    first = half * tiles
     return pl.pallas_call(
-        eliminate_kernel,
+        functools.partial(eliminate_kernel, len(into)),
         out_shape=jax.ShapeDtypeStruct((rows, cols), jnp.float32),
-        grid=(rows // tile,),
+        grid=(tiles,),
         in_specs=[
-            pl.BlockSpec((tile, cols), lambda i: (i, 0)),
-            pl.BlockSpec((tile, depth), lambda i: (i, 0)),
+            pl.BlockSpec((tile, cols), lambda i: (i + first, 0)),
+            pl.BlockSpec((tile, depth), lambda i: (i + first, 0)),
         ]
+        + [pl.BlockSpec(memory_space=pl.ANY) for _ in into]
         + [pl.BlockSpec(part.shape, lambda i: (0, 0), pipeline_mode=pl.Buffered(1)) for part in parts],
-        out_specs=pl.BlockSpec((tile, cols), lambda i: (i, 0)),
+        out_specs=pl.BlockSpec((tile, cols), lambda i: (i + first, 0)),
         scratch_shapes=[pltpu.VMEM((depth, cols), jnp.bfloat16)] * 2,
+        input_output_aliases={2: 0} if into else {},
         compiler_params=pltpu.CompilerParams(
-            vmem_limit_bytes=VMEM_LIMIT, dimension_semantics=("arbitrary",)
+            vmem_limit_bytes=32 * MIB, dimension_semantics=("arbitrary",)
         ),
         cost_estimate=pl.CostEstimate(
-            flops=6 * rows * cols * depth, bytes_accessed=12 * rows * cols, transcendentals=0
+            flops=3 * rows * cols * depth, bytes_accessed=6 * rows * cols, transcendentals=0
         ),
-    )(matrix, solved, *parts)
+    )(matrix, solved, *into, *parts)
 
 
 def pairs(count, offset):
@@ -385,17 +386,6 @@
 
 def partners(value, axis, count, offsets):
     return [value if d == 0 else lax.ppermute(value, axis, pairs(count, d)) for d in offsets]
-
-
-def all_rows(value, count):
-    both = jnp.stack(partners(value, "row", count, (0, 1)))
-    return jnp.concatenate(partners(both, "row", count, range(0, count, 2)))
-
-
-def line_rows(value, count):
-    mine = partners(value, "row", count, range(0, count, 2))
-    half = len(mine) // 2
-    return jnp.stack(mine[:half]), jnp.stack(mine[half:])
 
 
 def body(
@@ -451,14 +441,13 @@
         nbytes=size * modes * 8,
     )(runs, own, wanted)
     weighted_modes = tdot(own_modes, condensed_m, high)
+    inbox, weighted_modes = lax.optimization_barrier((inbox, weighted_modes))
     mode_outbox = call(
         functools.partial(pack_modes, grid, per_device),
         jax.ShapeDtypeStruct((grid.devices, grid.row_cap * per_device, SUBLANES, LANES), f32),
         [SMEM, SMEM, VMEM],
         nbytes=size * modes * 8,
     )(runs, own, weighted_modes)
-
-    inbox, mode_outbox = lax.optimization_barrier((inbox, mode_outbox))
     panel_row_count = PANEL // grid.rows
     panel_col_count = PANEL // grid.cols
     row_part, col_part, corner = call(
@@ -472,12 +461,13 @@
         nbytes=size * size * 4,
     )(row_tab, col_tab, inbox)
 
-    pieces = all_rows(corner, grid.rows)
+    pieces = jnp.stack(partners(corner, "row", grid.rows, (0, 1)))
+    pieces = jnp.concatenate(partners(pieces, "row", grid.rows, range(0, grid.rows, 2)))
     pieces, row_part, col_part, mode_outbox, inbox = lax.optimization_barrier(
         (pieces, row_part, col_part, mode_outbox, inbox)
     )
     pieces = jnp.stack(partners(pieces, "col", grid.cols, range(grid.cols)))
-    line = line_rows(row_part, grid.rows)
+    line = partners(row_part, "row", grid.rows, [1, *range(2, grid.rows, 2)])
     shifted = call(
         functools.partial(place_matrix, grid),
         jax.ShapeDtypeStruct((local_rows, local_cols), f32),
@@ -497,13 +487,12 @@
         flops=4 * PANEL**3,
         nbytes=PANEL * PANEL * 80,
     )(own, pieces)
+    inverse, rest = lax.optimization_barrier((inverse, line[1:]))
     solved = lax.dot_general(panel_cols, inverse, (((1,), (1,)), ((), ())), precision=highest)
-    solved, line = lax.optimization_barrier((solved, line))
-    panel_rows = []
-    for part in line:
-        for stack in partners(part, "row", grid.rows, (0, 1)):
-            panel_rows.append(stack.reshape(-1, local_cols))
-    solved, mode_inbox = lax.optimization_barrier((solved, mode_inbox))
+    panel_rows = [row_part, line[0]]
+    for part in rest:
+        panel_rows += partners(part, "row", grid.rows, (0, 1))
+    reduced_matrix = eliminate(shifted, solved, panel_rows, 0)
     modes_local = call(
         functools.partial(place_modes, grid, per_device),
         jax.ShapeDtypeStruct((mode_count, local_rows), f32),
@@ -512,11 +501,10 @@
     )(row_tab, mode_inbox)
     panel_modes = modes_local[:, :panel_row_count].T
     panel_modes = jnp.stack(partners(panel_modes, "row", grid.rows, (0, 1)))
-    panel_modes, shifted = lax.optimization_barrier((panel_modes, shifted))
+    panel_modes, reduced_matrix = lax.optimization_barrier((panel_modes, reduced_matrix))
     panel_modes = partners(panel_modes, "row", grid.rows, range(0, grid.rows, 2))
-    reduced_matrix = eliminate(shifted, solved, panel_rows)
-    panel_modes = jnp.concatenate(panel_modes)
-    panel_modes = jnp.concatenate([panel_modes[e] for e in grid.order])
+    reduced_matrix = eliminate(shifted, solved, panel_rows, 1, (reduced_matrix,))
+    panel_modes = jnp.concatenate(panel_modes).reshape(PANEL, -1)
     reduced_columns = modes_local - lax.dot_general(
         panel_modes, solved, (((0,), (1,)), ((), ())), precision=high
     )

time: 305 us -> 270 us (0.89)
  starting transfers between devices: 60.5 us -> 42.5 us
  Pallas kernels: 88.4 us -> 77.4 us
  other arithmetic: 11.1 us -> 2.54 us
  local copies, waits for them, and re-layouts: 14.2 us -> 22.1 us
  waiting for transfers between devices: 85.8 us -> 81.8 us
  matrix products: 43.5 us -> 39.7 us
    ppermute x19 -> x21, starting transfers between devices: 45.5 us -> 27.7 us  [partners(): lax.ppermute(value, axis, pairs(count, d))]
    unnamed x36 -> x42, local copies, waits for them, and re-layouts: 6.15 us -> 18.2 us
    ppermute x19 -> x21, waiting for transfers between devices: 52.5 us -> 43.4 us  [partners(): lax.ppermute(value, axis, pairs(count, d))]
    another operation x3 -> x1, other arithmetic: 5.36 us -> 0.01 us  [body(): pieces = jnp.stack(partners(corner, 'row', grid.rows, (0, 1)))]
    pallas_call x1 -> x2, Pallas kernels: 12.9 us -> 15.7 us  [eliminate(): pl.pallas_call(functools.partial(eliminate_kernel, len(into)), out_shape=...]
  transfers between devices with their start and end apart: 24 -> 26, of which waited for: 11 -> 7; matrix products, arithmetic and copies ran while one was open for 9% -> 4% of each run, Pallas kernels for 25% -> 25%
where the time goes in v3:
time: 270 us; the launch traced here: 267 us
  waiting for transfers between devices  81.8 us (30%)
  Pallas kernels  77.4 us (29%)
  starting transfers between devices  42.5 us (16%)
  matrix products  39.7 us (15%)
  local copies, waits for them, and re-layouts  22.1 us (8%)
    ppermute x21, waiting for transfers between devices, partners(): lax.ppermute(value, axis, pairs(count, d))  43.4 us
    ppermute x3, waiting for transfers between devices, exchange(): lax.ppermute(v, axis, pairs(count, d))  36.1 us
    pallas_call x1, Pallas kernels, body(): call(functools.partial(invert_corner, grid), jax.ShapeDtypeStruct((PANEL,...  31.2 us
    ppermute x21, starting transfers between devices, partners(): lax.ppermute(value, axis, pairs(count, d))  27.7 us
    dot_general x4, matrix products, tdot(): lax.dot_general(left, right, (((0,), (0,)), ((), ())), precision=precision)  23.3 us
    unnamed x42, local copies, waits for them, and re-layouts  18.2 us
    pallas_call x2, Pallas kernels, eliminate(): pl.pallas_call(functools.partial(eliminate_kernel, len(into)), out_shape=...  15.7 us
    pallas_call x1, Pallas kernels, body(): call(functools.partial(place_matrix, grid), jax.ShapeDtypeStruct((local_r...  11.1 us
  transfers between devices with their start and end apart: 26, of which 7 were waited for; matrix products, arithmetic and copies ran while one was open for 4% of the time, Pallas kernels for 25%

profile of v3, /device:TPU:0, one launch (start us, length us, event | category | flops | bytes accessed | tf_op | source)
XLA Modules:
  0.0 267.3 jit_solution(7649021576037657170)
XLA Ops:
  2.5 7.8 %fusion.4 = f32[1024,768]{1,0:T(8,128)S(1)} fusion(f32[1,1024,1024]{2,1,0:T(8,128)} %param.7, f32[1,1024,768]{2,1,0:T(8,128)S(1)} %copy-done), kind=kOutput, calls=%fused_computation.4 | convolution fusion | flops 4831838208 | bytes 10485760 | tf_op jit(solution)/shard_map/dot_general | solution.py:412
  12.0 5.2 %fusion.2 = f32[768,1024]{1,0:T(8,128)S(1)} fusion(f32[1024,768]{1,0:T(8,128)S(1)} %fusion.4, f32[1,1024,1024]{2,1,0:T(8,128)S(1)} %copy-done.18), kind=kOutput, calls=%fused_computation.2 | convolution fusion | flops 4831838208 | bytes 10485760 | tf_op jit(solution)/shard_map/dot_general | solution.py:25
  18.3 5.4 %fusion = f32[768,768]{1,0:T(8,128)} fusion(f32[768,1024]{1,0:T(8,128)S(1)} %fusion.2, f32[1024]{0:T(1024)S(1)} %bitcast.57), kind=kOutput, calls=%fused_computation | convolution fusion | flops 3624665088 | bytes 5509120 | tf_op jit(solution)/shard_map/dot_general | solution.py:25
  23.8 9.0 %fusion.7.a_ref = f32[768,768]{1,0:T(8,128)S(1)} fusion(f32[1,768,768]{2,1,0:T(8,128)} %param.9, f32[768,768]{1,0:T(8,128)} %fusion, f32[1024,768]{1,0:T(8,128)} %copy-done.13, f32[768]{0:T(1024)S(1)} %reduce.1), kind=kOutput, calls=%fused_computation.8 | convolution fusion | flops 3627417600 | bytes 10226688 | tf_op jit(solution)/shard_map/dot_general | solution.py:25
  32.8 2.8 %shard_map.86 = f32[32,18,8,128]{3,2,1,0:T(8,128)S(1)} custom-call(s32[32,6]{1,0:T(8,128)S(1)} %add_select_fusion.2.runs_ref, s32[1]{0:T(128)} %bitcast.own_ref, f32[768,768]{1,0:T(8,128)S(1)} %fusion.7.a_ref), custom_call_target="tpu_custom_call" | custom-call | bytes 4718592 | tf_op jit(solution)/shard_map/pallas_call | solution.py:417
  37.0 7.4 %all-to-all-start = ((f32[32,18,8,128]{3,2,1,0:T(8,128)}), f32[32,18,8,128]{3,2,1,0:T(8,128)}, u32[]{:S(2)}, u32[]{:S(2)}) async-start(f32[32,18,8,128]{3,2,1,0:T(8,128)} %copy-done.5), calls=%async_computation | async-start | bytes 4718592 | tf_op jit(solution)/shard_map/all_to_all | solution.py:423
  44.4 2.2 copy-done.8
  48.5 2.6 collective-permute-start.2
  52.8 28.2 %collective-permute-done.2 = f32[6,32,512]{2,1,0:T(8,128)S(1)} collective-permute-done((f32[6,32,512]{2,1,0:T(8,128)}, f32[6,32,512]{2,1,0:T(8,128)S(1)}, u32[]{:S(2)}, u32[]{:S(2)}) %collective-permute-start.2) | collective-permute-done | bytes 393248 | tf_op jit(solution)/shard_map/ppermute | solution.py:384
  81.0 7.9 %collective-permute-done = f32[6,32,512]{2,1,0:T(8,128)S(1)} collective-permute-done((f32[6,32,512]{2,1,0:T(8,128)S(1)}, f32[6,32,512]{2,1,0:T(8,128)S(1)}, u32[]{:S(2)}, u32[]{:S(2)}) %collective-permute-start) | collective-permute-done | bytes 393248 | tf_op jit(solution)/shard_map/ppermute | solution.py:384
  92.7 3.7 %fusion.16.y_ref = f32[512,768]{1,0:T(8,128)} fusion(f32[768,512]{1,0:T(8,128)S(1)} %shard_map.88, f32[768,768]{1,0:T(8,128)S(1)} %copy-done.12, f32[768]{0:T(1024)S(1)} %reduce.1), kind=kOutput, calls=%fused_computation.19 | convolution fusion | flops 1813708800 | bytes 5508096 | tf_op jit(solution)/shard_map/dot_general | solution.py:25
  96.4 2.4 all-to-all-done.in_ref
  98.7 7.5 %shard_map.89 = (f32[64,2048]{1,0:T(8,128)}, f32[1024,128]{1,0:T(8,128)S(1)}, f32[64,128]{1,0:T(8,128)S(1)}) custom-call(s32[32,3]{1,0:T(8,128)S(1)} %broadcast_add_fusion.row_tab, s32[32,6]{1,0:T(8,128)S(1)} %broadcast_add_fusion.1.col_tab, f32[32,18,8,128]{3,2,1,0:T(8,128)} %all-to-all-done.in_ref), custom_call_target="tpu_custom_call" | custom-call | bytes 2359296 | tf_op jit(solution)/shard_map/pallas_call | solution.py:453
  107.0 2.2 shard_map.90
  112.7 2.2 collective-permute-start.6
  115.0 5.3 %collective-permute-done.5 = f32[2,64,128]{2,1,0:T(8,128)S(1)} collective-permute-done((f32[2,64,128]{2,1,0:T(8,128)S(1)}, f32[2,64,128]{2,1,0:T(8,128)S(1)}, u32[]{:S(2)}, u32[]{:S(2)}) %collective-permute-start.5) | collective-permute-done | bytes 65568 | tf_op jit(solution)/shard_map/ppermute | solution.py:388
  123.8 11.1 %shard_map.91.matrix_ref = f32[1024,2048]{1,0:T(8,128)S(1)} custom-call(s32[32,3]{1,0:T(8,128)S(1)} %broadcast_add_fusion.row_tab, s32[32,6]{1,0:T(8,128)S(1)} %broadcast_add_fusion.1.col_tab, f32[32,18,8,128]{3,2,1,0:T(8,128)} %all-to-all-done.in_ref), custom_call_target="tpu_custom_call" | custom-call | bytes 16777216 | tf_op jit(solution)/shard_map/pallas_call | solution.py:471
  135.0 3.4 %copy-done.2 = f32[1024,2048]{1,0:T(8,128)} copy-done((f32[1024,2048]{1,0:T(8,128)}, f32[1024,2048]{1,0:T(8,128)S(1)}, u32[]{:S(2)}) %copy-start.2) | copy-done | bytes 8388632
  138.5 3.9 %all-to-all-start.1 = ((f32[32,12,8,128]{3,2,1,0:T(8,128)}), f32[32,12,8,128]{3,2,1,0:T(8,128)}, u32[]{:S(2)}, u32[]{:S(2)}) async-start(f32[32,12,8,128]{3,2,1,0:T(8,128)} %copy-done.6), calls=%async_computation.1 | async-start | bytes 3145728 | tf_op jit(solution)/shard_map/all_to_all | solution.py:481
  144.3 2.4 collective-permute-start.14
  150.2 35.3 %collective-permute-done.13.refs_2_.refs_3_ = f32[64,2048]{1,0:T(8,128)} collective-permute-done((f32[64,2048]{1,0:T(8,128)}, f32[64,2048]{1,0:T(8,128)}, u32[]{:S(2)}, u32[]{:S(2)}) %collective-permute-start.13) | collective-permute-done | bytes 524320 | tf_op jit(solution)/shard_map/ppermute | solution.py:388
  185.5 2.4 collective-permute-start.12
  187.9 31.2 %shard_map.92 = f32[512,512]{1,0:T(8,128)S(1)} custom-call(s32[1]{0:T(128)} %bitcast.own_ref, f32[4,8,64,128]{3,2,1,0:T(8,128)S(1)} %pad_maximum_fusion.1.pieces_ref), custom_call_target="tpu_custom_call" | custom-call | flops 536870912 | bytes 20971520 | tf_op jit(solution)/shard_map/pallas_call | solution.py:482
  220.2 4.8 %fusion.8.solved_ref = f32[1024,512]{1,0:T(8,128)} fusion(f32[512,512]{1,0:T(8,128)S(1)} %shard_map.92, f32[1024,128]{1,0:T(8,128)S(1)} %collective-permute-done.12, f32[1024,128]{1,0:T(8,128)S(1)} %collective-permute-done.11, f32[1024,128]{1,0:T(8,128)S(1)} %collective-permute-done.10, f32[1024,128]{1,0:T(8,128)S(1)} %copy-done.11), kind=kOutput, calls=%fused_computation.11 | convolution fusion | flops 3222798336 | bytes 5242880 | tf_op jit(solution)/shard_map/dot_general | solution.py:491
  225.1 5.0 %shard_map.93 = f32[128,1024]{1,0:T(8,128)S(1)} custom-call(s32[32,3]{1,0:T(8,128)S(1)} %broadcast_add_fusion.row_tab, f32[32,12,8,128]{3,2,1,0:T(8,128)} %all-to-all-done.1.in_ref), custom_call_target="tpu_custom_call" | custom-call | bytes 1048576 | tf_op jit(solution)/shard_map/pallas_call | solution.py:496
  230.9 3.4 %copy-done.3 = f32[1024,2048]{1,0:T(8,128)S(1)} copy-done((f32[1024,2048]{1,0:T(8,128)S(1)}, f32[1024,2048]{1,0:T(8,128)}, u32[]{:S(2)}) %copy-start.3) | copy-done | bytes 8388632
  234.3 7.9 %shard_map.94.refs_0_ = f32[1024,2048]{1,0:T(8,128)} custom-call(f32[1024,2048]{1,0:T(8,128)S(1)} %copy-done.3, f32[1024,512]{1,0:T(8,128)S(1)} %copy-done.4, f32[64,2048]{1,0:T(8,128)} %get-tuple-element.38.refs_0_.refs_1_, f32[64,2048]{1,0:T(8,128)} %collective-permute-done.17.refs_1_.refs_2_, f32[64,2048]{1,0:T(8,128)} %collective-permute-done.13.refs_2_.refs_3_, ...), custom_call_target="tpu_custom_call" | custom-call | flops 3221225472 | bytes 12582912 | tf_op jit(solution)/shard_map/pallas_call | solution.py:357
  242.2 5.9 %collective-permute-start.21 = (f32[2,64,128]{1,2,0:T(8,128)S(1)}, f32[2,64,128]{1,2,0:T(8,128)S(1)}, u32[]{:S(2)}, u32[]{:S(2)}) collective-permute-start(f32[2,64,128]{1,2,0:T(8,128)S(1)} %pad_maximum_fusion.3), channel_id=1, source_target_pairs={{0,8},{4,12},{8,0},{12,4},{16,24},{20,28},{24,16},{28,20},{1,9},{5... | collective-permute-start | bytes 196616 | tf_op jit(solution)/shard_map/ppermute | solution.py:388
  248.1 2.4 collective-permute-start.23
  250.5 7.9 %shard_map.95 = f32[1024,2048]{1,0:T(8,128)} custom-call(f32[1024,2048]{1,0:T(8,128)S(1)} %copy-done.3, f32[1024,512]{1,0:T(8,128)S(1)} %copy-done.4, f32[1024,2048]{1,0:T(8,128)} %shard_map.94.refs_0_, f32[64,2048]{1,0:T(8,128)} %get-tuple-element.38.refs_0_.refs_1_, ...), custom_call_target="tpu_custom_call", output_to_operand_aliasing={{}: (2, {})} | custom-call | flops 3221225472 | bytes 12582912 | tf_op jit(solution)/shard_map/pallas_call | solution.py:357
  258.4 2.6 collective-permute-done.22
  263.4 3.7 %convolution_subtract_fusion = f32[128,1024]{1,0:T(8,128)} fusion(f32[128,1024]{1,0:T(8,128)} %copy-done.9, f32[512,128]{1,0:T(8,128)S(1)} %bitcast.47, f32[1024,512]{1,0:T(8,128)} %fusion.8.solved_ref), kind=kOutput, calls=%fused_computation.22 | convolution fusion | flops 402784256 | bytes 3407872 | tf_op jit(solution)/shard_map/dot_general | solution.py:508
  (106 shorter events, 31.0 us)
Async XLA Ops:
  2.5 9.5 %copy-start.18 = (f32[1,1024,1024]{2,1,0:T(8,128)S(1)}, f32[1,1024,1024]{2,1,0:T(8,128)}, u32[]{:S(2)}) copy-start(f32[1,1024,1024]{2,1,0:T(8,128)} %param.7) | copy-start | bytes 12582916
  12.0 6.3 %copy-start.16 = (f32[1,1024]{1,0:T(1,128)S(1)}, f32[1,1024]{1,0:T(1,128)}, u32[]{:S(2)}) copy-start(f32[1,1024]{1,0:T(1,128)} %param.10) | copy-start | bytes 12292
  37.0 61.8 %all-to-all-start = ((f32[32,18,8,128]{3,2,1,0:T(8,128)}), f32[32,18,8,128]{3,2,1,0:T(8,128)}, u32[]{:S(2)}, u32[]{:S(2)}) async-start(f32[32,18,8,128]{3,2,1,0:T(8,128)} %copy-done.5), calls=%async_computation | async-start | bytes 4718592 | tf_op jit(solution)/shard_map/all_to_all | solution.py:423
  48.5 32.5 %collective-permute-start.2 = (f32[6,32,512]{2,1,0:T(8,128)}, f32[6,32,512]{2,1,0:T(8,128)S(1)}, u32[]{:S(2)}, u32[]{:S(2)}) collective-permute-start(f32[6,32,512]{2,1,0:T(8,128)} %get-tuple-element.49), channel_id=1, source_target_pairs={{0,3},{1,2},{2,1},{3,0},{4,7},{5,6},{6,5},{7,4},{8,11},{9,10},{10,... | collective-permute-start | bytes 1179656 | tf_op jit(solution)/shard_map/ppermute | solution.py:384
  51.1 37.8 %collective-permute-start = (f32[6,32,512]{2,1,0:T(8,128)S(1)}, f32[6,32,512]{2,1,0:T(8,128)S(1)}, u32[]{:S(2)}, u32[]{:S(2)}) collective-permute-start(f32[6,32,512]{2,1,0:T(8,128)S(1)} %get-tuple-element.51), channel_id=1, source_target_pairs={{0,1},{1,0},{2,3},{3,2},{4,5},{5,4},{6,7},{7,6},{8,9},{9,8},{10,11... | collective-permute-start | bytes 1179656 | tf_op jit(solution)/shard_map/ppermute | solution.py:384
  51.7 37.2 %collective-permute-start.1 = (f32[6,32,512]{2,1,0:T(8,128)S(1)}, f32[6,32,512]{2,1,0:T(8,128)S(1)}, u32[]{:S(2)}, u32[]{:S(2)}) collective-permute-start(f32[6,32,512]{2,1,0:T(8,128)S(1)} %get-tuple-element.50), channel_id=1, source_target_pairs={{0,2},{1,3},{2,0},{3,1},{4,6},{5,7},{6,4},{7,5},{8,10},{9,11},{10,... | collective-permute-start | bytes 1179656 | tf_op jit(solution)/shard_map/ppermute | solution.py:384
  98.7 8.3 %copy-start.7 = (f32[512,768]{1,0:T(8,128)S(1)}, f32[512,768]{1,0:T(8,128)}, u32[]{:S(2)}) copy-start(f32[512,768]{1,0:T(8,128)} %fusion.16.y_ref) | copy-start | bytes 4718596
  107.0 3.4 %collective-permute-start.3 = (f32[64,128]{1,0:T(8,128)S(1)}, f32[64,128]{1,0:T(8,128)S(1)}, u32[]{:S(2)}, u32[]{:S(2)}) collective-permute-start(f32[64,128]{1,0:T(8,128)S(1)} %get-tuple-element.27), channel_id=1, source_target_pairs={{0,4},{4,0},{8,12},{12,8},{16,20},{20,16},{24,28},{28,24},{1,5},{5... | collective-permute-start | bytes 98312 | tf_op jit(solution)/shard_map/ppermute | solution.py:388
  110.4 4.6 %collective-permute-start.4 = (f32[2,64,128]{2,1,0:T(8,128)S(1)}, f32[2,64,128]{2,1,0:T(8,128)S(1)}, u32[]{:S(2)}, u32[]{:S(2)}) collective-permute-start(f32[2,64,128]{2,1,0:T(8,128)S(1)} %pad_maximum_fusion.4), channel_id=1, source_target_pairs={{0,8},{4,12},{8,0},{12,4},{16,24},{20,28},{24,16},{28,20},{1,9},{5... | collective-permute-start | bytes 196616 | tf_op jit(solution)/shard_map/ppermute | solution.py:388
  112.0 8.3 %collective-permute-start.5 = (f32[2,64,128]{2,1,0:T(8,128)S(1)}, f32[2,64,128]{2,1,0:T(8,128)S(1)}, u32[]{:S(2)}, u32[]{:S(2)}) collective-permute-start(f32[2,64,128]{2,1,0:T(8,128)S(1)} %pad_maximum_fusion.4), channel_id=1, source_target_pairs={{0,16},{4,20},{8,24},{12,28},{16,0},{20,4},{24,8},{28,12},{1,17},{... | collective-permute-start | bytes 196616 | tf_op jit(solution)/shard_map/ppermute | solution.py:388
  112.7 7.6 %collective-permute-start.6 = (f32[2,64,128]{2,1,0:T(8,128)S(1)}, f32[2,64,128]{2,1,0:T(8,128)S(1)}, u32[]{:S(2)}, u32[]{:S(2)}) collective-permute-start(f32[2,64,128]{2,1,0:T(8,128)S(1)} %pad_maximum_fusion.4), channel_id=1, source_target_pairs={{0,24},{4,28},{8,16},{12,20},{16,8},{20,12},{24,0},{28,4},{1,25},{... | collective-permute-start | bytes 196616 | tf_op jit(solution)/shard_map/ppermute | solution.py:388
  120.3 18.1 %collective-permute-start.7 = (f32[8,64,128]{2,1,0:T(8,128)S(1)}, f32[8,64,128]{2,1,0:T(8,128)S(1)}, u32[]{:S(2)}, u32[]{:S(2)}) collective-permute-start(f32[8,64,128]{2,1,0:T(8,128)S(1)} %constant_dynamic-update-slice_fusion), channel_id=1, source_target_pairs={{0,1},{1,0},{2,3},{3,2},{4,5},{5,4},{6,7},{7,6},{8,9},{9,8},{10,11... | collective-permute-start | bytes 786440 | tf_op jit(solution)/shard_map/ppermute | solution.py:388
  120.8 17.6 %collective-permute-start.8 = (f32[8,64,128]{2,1,0:T(8,128)S(1)}, f32[8,64,128]{2,1,0:T(8,128)S(1)}, u32[]{:S(2)}, u32[]{:S(2)}) collective-permute-start(f32[8,64,128]{2,1,0:T(8,128)S(1)} %constant_dynamic-update-slice_fusion), channel_id=1, source_target_pairs={{0,2},{1,3},{2,0},{3,1},{4,6},{5,7},{6,4},{7,5},{8,10},{9,11},{10,... | collective-permute-start | bytes 786440 | tf_op jit(solution)/shard_map/ppermute | solution.py:388
  122.6 15.7 %collective-permute-start.9 = (f32[8,64,128]{2,1,0:T(8,128)S(1)}, f32[8,64,128]{2,1,0:T(8,128)S(1)}, u32[]{:S(2)}, u32[]{:S(2)}) collective-permute-start(f32[8,64,128]{2,1,0:T(8,128)S(1)} %constant_dynamic-update-slice_fusion), channel_id=1, source_target_pairs={{0,3},{1,2},{2,1},{3,0},{4,7},{5,6},{6,5},{7,4},{8,11},{9,10},{10,... | collective-permute-start | bytes 786440 | tf_op jit(solution)/shard_map/ppermute | solution.py:388
  138.4 8.5 %copy-start.11 = (f32[1024,128]{1,0:T(8,128)S(1)}, f32[1024,128]{1,0:T(8,128)}, u32[]{:S(2)}) copy-start(f32[1024,128]{1,0:T(8,128)} %copy-done.10) | copy-start | bytes 1572868
  138.5 86.6 %all-to-all-start.1 = ((f32[32,12,8,128]{3,2,1,0:T(8,128)}), f32[32,12,8,128]{3,2,1,0:T(8,128)}, u32[]{:S(2)}, u32[]{:S(2)}) async-start(f32[32,12,8,128]{3,2,1,0:T(8,128)} %copy-done.6), calls=%async_computation.1 | async-start | bytes 3145728 | tf_op jit(solution)/shard_map/all_to_all | solution.py:481
  142.4 43.1 %collective-permute-start.13 = (f32[64,2048]{1,0:T(8,128)}, f32[64,2048]{1,0:T(8,128)}, u32[]{:S(2)}, u32[]{:S(2)}) collective-permute-start(f32[64,2048]{1,0:T(8,128)} %get-tuple-element.38.refs_0_.refs_1_), channel_id=1, source_target_pairs={{0,8},{4,12},{8,0},{12,4},{16,24},{20,28},{24,16},{28,20},{1,9},{5... | collective-permute-start | bytes 1572872 | tf_op jit(solution)/shard_map/ppermute | solution.py:388
  144.3 74.8 %collective-permute-start.14 = (f32[64,2048]{1,0:T(8,128)}, f32[64,2048]{1,0:T(8,128)}, u32[]{:S(2)}, u32[]{:S(2)}) collective-permute-start(f32[64,2048]{1,0:T(8,128)} %get-tuple-element.38.refs_0_.refs_1_), channel_id=1, source_target_pairs={{0,16},{4,20},{8,24},{12,28},{16,0},{20,4},{24,8},{28,12},{1,17},{... | collective-permute-start | bytes 1572872 | tf_op jit(solution)/shard_map/ppermute | solution.py:388
  146.7 72.5 %collective-permute-start.15 = (f32[64,2048]{1,0:T(8,128)}, f32[64,2048]{1,0:T(8,128)}, u32[]{:S(2)}, u32[]{:S(2)}) collective-permute-start(f32[64,2048]{1,0:T(8,128)} %get-tuple-element.38.refs_0_.refs_1_), channel_id=1, source_target_pairs={{0,24},{4,28},{8,16},{12,20},{16,8},{20,12},{24,0},{28,4},{1,25},{... | collective-permute-start | bytes 1572872 | tf_op jit(solution)/shard_map/ppermute | solution.py:388
  146.8 72.9 %collective-permute-start.10 = (f32[1024,128]{1,0:T(8,128)S(1)}, f32[1024,128]{1,0:T(8,128)S(1)}, u32[]{:S(2)}, u32[]{:S(2)}) collective-permute-start(f32[1024,128]{1,0:T(8,128)S(1)} %copy-done.11), channel_id=1, source_target_pairs={{0,1},{1,0},{2,3},{3,2},{4,5},{5,4},{6,7},{7,6},{8,9},{9,8},{10,11... | collective-permute-start | bytes 1572872 | tf_op jit(solution)/shard_map/ppermute | solution.py:388
  148.7 71.1 %collective-permute-start.11 = (f32[1024,128]{1,0:T(8,128)S(1)}, f32[1024,128]{1,0:T(8,128)S(1)}, u32[]{:S(2)}, u32[]{:S(2)}) collective-permute-start(f32[1024,128]{1,0:T(8,128)S(1)} %copy-done.11), channel_id=1, source_target_pairs={{0,2},{1,3},{2,0},{3,1},{4,6},{5,7},{6,4},{7,5},{8,10},{9,11},{10,... | collective-permute-start | bytes 1572872 | tf_op jit(solution)/shard_map/ppermute | solution.py:388
  185.5 34.7 %collective-permute-start.12 = (f32[1024,128]{1,0:T(8,128)S(1)}, f32[1024,128]{1,0:T(8,128)S(1)}, u32[]{:S(2)}, u32[]{:S(2)}) collective-permute-start(f32[1024,128]{1,0:T(8,128)S(1)} %copy-done.11), channel_id=1, source_target_pairs={{0,3},{1,2},{2,1},{3,0},{4,7},{5,6},{6,5},{7,4},{8,11},{9,10},{10,... | collective-permute-start | bytes 1572872 | tf_op jit(solution)/shard_map/ppermute | solution.py:388
  219.1 11.1 %collective-permute-start.17 = (f32[64,2048]{1,0:T(8,128)}, f32[64,2048]{1,0:T(8,128)}, u32[]{:S(2)}, u32[]{:S(2)}) collective-permute-start(f32[64,2048]{1,0:T(8,128)} %get-tuple-element.38.refs_0_.refs_1_), channel_id=1, source_target_pairs={{0,4},{4,0},{8,12},{12,8},{16,20},{20,16},{24,28},{28,24},{1,5},{5... | collective-permute-start | bytes 1572872 | tf_op jit(solution)/shard_map/ppermute | solution.py:388
  219.2 11.1 %collective-permute-start.18 = (f32[64,2048]{1,0:T(8,128)}, f32[64,2048]{1,0:T(8,128)}, u32[]{:S(2)}, u32[]{:S(2)}) collective-permute-start(f32[64,2048]{1,0:T(8,128)} %collective-permute-done.13.refs_2_.refs_3_), channel_id=1, source_target_pairs={{0,4},{4,0},{8,12},{12,8},{16,20},{20,16},{24,28},{28,24},{1,5},{5... | collective-permute-start | bytes 1572872 | tf_op jit(solution)/shard_map/ppermute | solution.py:388
  219.7 10.6 %collective-permute-start.19 = (f32[64,2048]{1,0:T(8,128)}, f32[64,2048]{1,0:T(8,128)}, u32[]{:S(2)}, u32[]{:S(2)}) collective-permute-start(f32[64,2048]{1,0:T(8,128)} %collective-permute-done.14.refs_4_.refs_5_), channel_id=1, source_target_pairs={{0,4},{4,0},{8,12},{12,8},{16,20},{20,16},{24,28},{28,24},{1,5},{5... | collective-permute-start | bytes 1572872 | tf_op jit(solution)/shard_map/ppermute | solution.py:388
  219.8 11.1 %collective-permute-start.20 = (f32[64,2048]{1,0:T(8,128)}, f32[64,2048]{1,0:T(8,128)}, u32[]{:S(2)}, u32[]{:S(2)}) collective-permute-start(f32[64,2048]{1,0:T(8,128)} %collective-permute-done.15.refs_6_.refs_7_), channel_id=1, source_target_pairs={{0,4},{4,0},{8,12},{12,8},{16,20},{20,16},{24,28},{28,24},{1,5},{5... | collective-permute-start | bytes 1572872 | tf_op jit(solution)/shard_map/ppermute | solution.py:388
  225.1 5.8 %copy-start.4 = (f32[1024,512]{1,0:T(8,128)S(1)}, f32[1024,512]{1,0:T(8,128)}, u32[]{:S(2)}) copy-start(f32[1024,512]{1,0:T(8,128)} %fusion.8.solved_ref) | copy-start | bytes 6291460
  230.1 12.0 %collective-permute-start.16 = (f32[64,128]{0,1:T(8,128)S(1)}, f32[64,128]{0,1:T(8,128)S(1)}, u32[]{:S(2)}, u32[]{:S(2)}) collective-permute-start(f32[64,128]{0,1:T(8,128)S(1)} %get-tuple-element.53), channel_id=1, source_target_pairs={{0,4},{4,0},{8,12},{12,8},{16,20},{20,16},{24,28},{28,24},{1,5},{5... | collective-permute-start | bytes 98312 | tf_op jit(solution)/shard_map/ppermute | solution.py:388
  242.2 16.2 %collective-permute-start.21 = (f32[2,64,128]{1,2,0:T(8,128)S(1)}, f32[2,64,128]{1,2,0:T(8,128)S(1)}, u32[]{:S(2)}, u32[]{:S(2)}) collective-permute-start(f32[2,64,128]{1,2,0:T(8,128)S(1)} %pad_maximum_fusion.3), channel_id=1, source_target_pairs={{0,8},{4,12},{8,0},{12,4},{16,24},{20,28},{24,16},{28,20},{1,9},{5... | collective-permute-start | bytes 196616 | tf_op jit(solution)/shard_map/ppermute | solution.py:388
  248.1 12.9 %collective-permute-start.22 = (f32[2,64,128]{1,2,0:T(8,128)S(1)}, f32[2,64,128]{1,2,0:T(8,128)S(1)}, u32[]{:S(2)}, u32[]{:S(2)}) collective-permute-start(f32[2,64,128]{1,2,0:T(8,128)S(1)} %pad_maximum_fusion.3), channel_id=1, source_target_pairs={{0,16},{4,20},{8,24},{12,28},{16,0},{20,4},{24,8},{28,12},{1,17},{... | collective-permute-start | bytes 196616 | tf_op jit(solution)/shard_map/ppermute | solution.py:388
  248.1 12.9 %collective-permute-start.23 = (f32[2,64,128]{1,2,0:T(8,128)S(1)}, f32[2,64,128]{1,2,0:T(8,128)S(1)}, u32[]{:S(2)}, u32[]{:S(2)}) collective-permute-start(f32[2,64,128]{1,2,0:T(8,128)S(1)} %pad_maximum_fusion.3), channel_id=1, source_target_pairs={{0,24},{4,28},{8,16},{12,20},{16,8},{20,12},{24,0},{28,4},{1,25},{... | collective-permute-start | bytes 196616 | tf_op jit(solution)/shard_map/ppermute | solution.py:388
  261.0 6.1 %copy-start.1 = (f32[1,1024,768]{2,1,0:T(8,128)S(1)}, f32[1,1024,768]{2,1,0:T(8,128)}, u32[]{:S(2)}) copy-start(f32[1,1024,768]{2,1,0:T(8,128)} %param.8) | copy-start | bytes 9437188
  (13 other events, 25.5 us)
